TPU v7x, 32 devices: a whole 2x2x4 slice. The times are simulated.
32 devices in a mesh: expert: 2 (over x), shard: 16 (over z, y, core).
Axes of the slice: x: 2, y: 2, z: 4, core: 2. Of those that a mesh axis runs over, the one named last changes fastest.
Arguments:
- tokens: bfloat16 [16, 512, 768], P('shard', 'expert'), may hold values from -32 to 32
- segment_ids: int32 [16, 512], P('shard'), may hold values from 0 to 3, never falling along the last dimension, each value on 1 to 256 neighbouring positions
- routes: int32 [16, 512, 2], P('shard', 'expert'), may hold values from 0 to 11, as said below
- earlier_logits: float32 [16, 512, 12], P('shard', 'expert'), may hold values from -3 to 3
- out_cotangent: bfloat16 [16, 512, 768], P('shard', 'expert'), may hold values from -6 to 6
- query_weight: bfloat16 [768, 768], P('shard'), may hold values from -0.3125 to 0.3125
- key_weight: bfloat16 [768, 768], P('shard'), may hold values from -0.3125 to 0.3125
- value_weight: bfloat16 [768, 768], P('shard'), may hold values from -0.21875 to 0.21875
- output_weight: bfloat16 [768, 768], P('shard'), may hold values from -0.875 to 0.875
- router_weight: bfloat16 [768, 12], P('shard'), may hold values from -0.109375 to 0.109375
- const_vectors: bfloat16 [768, 2], P('shard'), may hold values from -4 to 4
- attn_gain: bfloat16 [768], P('shard'), may hold values from 0.5 to 1.5
- moe_gain: bfloat16 [768], P('shard'), may hold values from 0.5 to 1.5
- gate_weight: bfloat16 [8, 768, 2048], P('expert', 'shard'), may hold values from -0.21875 to 0.21875
- up_weight: bfloat16 [8, 768, 2048], P('expert', 'shard'), may hold values from -0.21875 to 0.21875
- down_weight: bfloat16 [8, 2048, 768], P('expert', 'shard'), may hold values from -0.125 to 0.125
Outputs:
- layer_out: bfloat16 [16, 512, 768], P('shard', 'expert')
- tokens_grad: float32 [16, 512, 768], P('shard', 'expert')
- prior_logits_gradient: float32 [16, 512, 12], P('shard', 'expert')
- query_grad: float32 [768, 768], P('shard')
- key_grad: float32 [768, 768], P('shard')
- value_grad: float32 [768, 768], P('shard')
- output_grad: float32 [768, 768], P('shard')
- router_grad: float32 [768, 12], P('shard')
- const_grad: float32 [768, 2], P('shard')
- attn_gain_grad: float32 [768], P('shard')
- moe_gain_grad: float32 [768], P('shard')
- gate_grad: float32 [8, 768, 2048], P('expert', 'shard')
- up_grad: float32 [8, 768, 2048], P('expert', 'shard')
- down_grad: float32 [8, 2048, 768], P('expert', 'shard')
Inputs may be any that keep to these rules, and one draw needn't show every extreme that they name: `routes`: each token names two different experts. In each aligned block of 256 positions of a sequence no expert is named more than 64 times, and some expert below 8 exactly 64 times. `segment_ids`: ids never fall along a sequence; each document has at most 256 positions, and one has exactly 256.
All inputs are finite; a program needn't handle non-finite values.
Results may differ from a plain program's by a relative error of at most 0.035.
Values may be sent and summed in bfloat16 or wider, within the bound.
No kernel may reach another device: no remote copies, remote signals or barrier semaphores. Data moves between devices by JAX's collectives and lax.ppermute only.
A program may use at most 128 MiB of HBM per device.

v0:
```python
import math

import jax
import jax.numpy as jnp
from jax import lax
from jax.experimental import pallas as pl
from jax.experimental.pallas import tpu as pltpu
from jax.sharding import PartitionSpec as P

HEADS = 12
EXPERTS = 8
CAP = 64


norm_eps = 1e-06
masked_fill = -1e30


def rotary(values, positions, direction):
    dims_in = values.shape
    heads_view = values.reshape(dims_in[:-1] + (HEADS, dims_in[-1] // HEADS))
    half_size = heads_view.shape[-1] // 2
    frequency = jnp.exp(
        jnp.arange(half_size, dtype=jnp.float32) * (-2.0 * math.log(10000.0) / (2 * half_size))
    )
    angles = positions.astype(jnp.float32)[:, None] * frequency[None, :]
    cosine = jnp.cos(angles)[:, None, :]
    sine_part = direction * jnp.sin(angles)[:, None, :]
    first_half = heads_view[..., :half_size]
    second_half = heads_view[..., half_size:]
    turned = jnp.concatenate(
        [
            first_half * cosine - second_half * sine_part,
            second_half * cosine + first_half * sine_part,
        ],
        axis=-1,
    )
    return turned.reshape(dims_in)


def rms_parts(values):
    inverse = lax.rsqrt(jnp.mean(values * values, axis=-1, keepdims=True) + norm_eps)
    return (values * inverse, inverse)


def rms_back(grad_scaled, values, inverse):
    inner_mean = jnp.mean(grad_scaled * values, axis=-1, keepdims=True)
    return inverse * grad_scaled - values * inverse * inverse * inverse * inner_mean


def block_scores(query_heads, keys_all, segment_row, query_pos, query_seg, key_start, width_block):
    key_block = lax.dynamic_slice_in_dim(keys_all, key_start, width_block, 0)
    key_heads = key_block.reshape(width_block, HEADS, key_block.shape[-1] // HEADS)
    raw_scores = jnp.einsum(
        "qhd,khd->hqk", query_heads, key_heads, preferred_element_type=jnp.float32
    )
    scaled = raw_scores * key_heads.shape[-1] ** (-0.5)
    key_pos = key_start + jnp.arange(width_block, dtype=jnp.int32)
    key_seg = lax.dynamic_slice_in_dim(segment_row, key_start, width_block, 0)
    allowed = (key_pos[None, :] <= query_pos[:, None]) & (key_seg[None, :] == query_seg[:, None])
    return (scaled, allowed[None], key_heads)


def attend_forward(query_rot, keys_all, values_all, segment_row, offset, block_count, width_block):
    row_count = query_rot.shape[0]
    query_heads = query_rot.reshape(row_count, HEADS, -1)
    query_pos = offset + jnp.arange(row_count, dtype=jnp.int32)
    query_seg = lax.dynamic_slice_in_dim(segment_row, offset, row_count, 0)

    def gather_stats(number, state_pair):
        running_max, running_sum = state_pair
        scaled, allowed, key_heads = block_scores(
            query_heads,
            keys_all,
            segment_row,
            query_pos,
            query_seg,
            number * width_block,
            width_block,
        )
        masked = jnp.where(allowed, scaled, masked_fill)
        new_max = jnp.maximum(running_max, jnp.max(masked, axis=-1))
        exp_terms = jnp.where(allowed, jnp.exp(masked - new_max[..., None]), 0.0)
        return (new_max, running_sum * jnp.exp(running_max - new_max) + jnp.sum(exp_terms, axis=-1))

    start_max = jnp.full((HEADS, row_count), masked_fill, jnp.float32)
    start_sum = jnp.zeros((HEADS, row_count), jnp.float32)
    final_max, final_sum = lax.fori_loop(0, block_count, gather_stats, (start_max, start_sum))
    log_total = final_max + jnp.log(final_sum)

    def gather_output(number, running_out):
        key_start = number * width_block
        scaled, allowed, key_heads = block_scores(
            query_heads, keys_all, segment_row, query_pos, query_seg, key_start, width_block
        )
        weights = jnp.where(allowed, jnp.exp(scaled - log_total[..., None]), 0.0).astype(
            jnp.bfloat16
        )
        value_heads = lax.dynamic_slice_in_dim(values_all, key_start, width_block, 0).reshape(
            width_block, HEADS, -1
        )
        return running_out + jnp.einsum(
            "hqk,khd->qhd", weights, value_heads, preferred_element_type=jnp.float32
        )

    start_out = jnp.zeros((row_count, HEADS, query_heads.shape[-1]), jnp.float32)
    attention_output = lax.fori_loop(0, block_count, gather_output, start_out)
    return (attention_output.reshape(row_count, -1), log_total)


def attend_backward(
    query_rot,
    keys_all,
    values_all,
    segment_row,
    log_total,
    delta_sum,
    grad_low,
    offset,
    block_count,
    width_block,
):
    row_count = query_rot.shape[0]
    key_total = keys_all.shape[0]
    model_width = keys_all.shape[1]
    query_heads = query_rot.reshape(row_count, HEADS, -1)
    grad_heads = grad_low.reshape(row_count, HEADS, -1)
    query_pos = offset + jnp.arange(row_count, dtype=jnp.int32)
    query_seg = lax.dynamic_slice_in_dim(segment_row, offset, row_count, 0)
    score_scale = query_heads.shape[-1] ** (-0.5)

    def block_parts(number):
        key_start = number * width_block
        scaled, allowed, key_heads = block_scores(
            query_heads, keys_all, segment_row, query_pos, query_seg, key_start, width_block
        )
        prob_block = jnp.where(allowed, jnp.exp(scaled - log_total[..., None]), 0.0)
        value_heads = lax.dynamic_slice_in_dim(values_all, key_start, width_block, 0).reshape(
            width_block, HEADS, -1
        )
        grad_probs = jnp.einsum(
            "qhd,khd->hqk", grad_heads, value_heads, preferred_element_type=jnp.float32
        )
        grad_raw = (prob_block * (grad_probs - delta_sum[..., None]) * score_scale).astype(
            jnp.bfloat16
        )
        return (key_start, key_heads, prob_block, grad_raw)

    start_query = jnp.zeros((row_count, HEADS, query_heads.shape[-1]), jnp.float32)

    def accumulate(number, state_all):
        grad_query, grad_keys, grad_values = state_all
        key_start, key_heads, prob_block, grad_raw = block_parts(number)
        grad_query = grad_query + jnp.einsum(
            "hqk,khd->qhd", grad_raw, key_heads, preferred_element_type=jnp.float32
        )
        key_part = jnp.einsum(
            "hqk,qhd->khd", grad_raw, query_heads, preferred_element_type=jnp.float32
        )
        value_part = jnp.einsum(
            "hqk,qhd->khd",
            prob_block.astype(jnp.bfloat16),
            grad_heads,
            preferred_element_type=jnp.float32,
        )
        grad_keys = lax.dynamic_update_slice_in_dim(
            grad_keys, key_part.reshape(width_block, -1), key_start, 0
        )
        grad_values = lax.dynamic_update_slice_in_dim(
            grad_values, value_part.reshape(width_block, -1), key_start, 0
        )
        return (grad_query, grad_keys, grad_values)

    start_state = (
        start_query,
        jnp.zeros((key_total, model_width), jnp.float32),
        jnp.zeros((key_total, model_width), jnp.float32),
    )
    grad_query, grad_keys, grad_values = lax.fori_loop(0, block_count, accumulate, start_state)
    return (grad_query.reshape(row_count, -1), grad_keys, grad_values)


def body(
    tokens,
    segment_ids,
    routes,
    earlier_logits,
    out_cotangent,
    query_weight,
    key_weight,
    value_weight,
    output_weight,
    router_weight,
    const_vectors,
    attn_gain,
    moe_gain,
    gate_weight,
    up_weight,
    down_weight,
):
    (
        query_weight_wide,
        key_weight_wide,
        value_weight_wide,
        output_weight_wide,
        router_weight_wide,
        const_full,
        gain_attn,
        gain_moe,
    ) = (
        lax.all_gather(query_weight, "shard", axis=0, tiled=True),
        lax.all_gather(key_weight, "shard", axis=0, tiled=True),
        lax.all_gather(value_weight, "shard", axis=0, tiled=True),
        lax.all_gather(output_weight, "shard", axis=0, tiled=True),
        lax.all_gather(router_weight, "shard", axis=0, tiled=True),
        lax.all_gather(const_vectors, "shard", axis=0, tiled=True),
        lax.all_gather(attn_gain, "shard", axis=0, tiled=True),
        lax.all_gather(moe_gain, "shard", axis=0, tiled=True),
    )
    gate_full, up_full, down_full = (
        lax.all_gather(gate_weight, "shard", axis=1, tiled=True),
        lax.all_gather(up_weight, "shard", axis=1, tiled=True),
        lax.all_gather(down_weight, "shard", axis=1, tiled=True),
    )
    seq_count, pos_count, model_width = tokens.shape
    expert_pos = lax.axis_index("expert")
    offset = expert_pos * pos_count
    width_block = math.gcd(pos_count, 128)
    block_count = (expert_pos + 1) * (pos_count // width_block)
    positions = offset + jnp.arange(pos_count, dtype=jnp.int32)
    tokens_wide = tokens.astype(jnp.float32)
    scaled_one, inverse_one = rms_parts(tokens_wide)
    attn_gain_wide = gain_attn.astype(jnp.float32)
    normalized_first = (scaled_one * attn_gain_wide).astype(jnp.bfloat16)
    query_unrotated = jnp.einsum(
        "ibg,gv->ibv", normalized_first, query_weight_wide, preferred_element_type=jnp.float32
    )
    key_unrotated = jnp.einsum(
        "ibg,gv->ibv", normalized_first, key_weight_wide, preferred_element_type=jnp.float32
    )
    value_projected = jnp.einsum(
        "ibg,gv->ibv", normalized_first, value_weight_wide, preferred_element_type=jnp.float32
    )
    query_rot = rotary(query_unrotated, positions, 1.0).astype(jnp.bfloat16)
    key_rot = rotary(key_unrotated, positions, 1.0).astype(jnp.bfloat16)
    value_low = value_projected.astype(jnp.bfloat16)
    keys_all, values_all = (
        lax.all_gather(key_rot, "expert", axis=1, tiled=True),
        lax.all_gather(value_low, "expert", axis=1, tiled=True),
    )

    def forward_one(packed):
        return attend_forward(
            packed[0], packed[1], packed[2], packed[3], offset, block_count, width_block
        )

    attention_output, log_total = lax.map(
        forward_one, (query_rot, keys_all, values_all, segment_ids)
    )
    attention_output_narrow = attention_output.astype(jnp.bfloat16)
    projected_rows = jnp.einsum(
        "ibg,gv->ibv",
        attention_output_narrow,
        output_weight_wide,
        preferred_element_type=jnp.float32,
    )
    middle = tokens_wide + projected_rows
    scaled_two, inverse_two = rms_parts(middle)
    moe_gain_wide = gain_moe.astype(jnp.float32)
    normed_two = scaled_two * moe_gain_wide
    normalized_narrow = normed_two.astype(jnp.bfloat16)
    router_logits = (
        jnp.einsum(
            "ibg,gv->ibv", normalized_narrow, router_weight_wide, preferred_element_type=jnp.float32
        )
        + earlier_logits
    )
    chosen = jnp.take_along_axis(router_logits, routes, axis=-1)
    gate_probs = jax.nn.softmax(chosen, axis=-1)
    slot_count = seq_count * CAP
    route_entries = routes.reshape(seq_count, pos_count * 2)
    one_hot = (route_entries[..., None] == jnp.arange(EXPERTS, dtype=jnp.int32)).astype(jnp.int32)
    entry_ranks = jnp.cumsum(one_hot, axis=1) - one_hot
    slot_rank = jnp.sum(entry_ranks * one_hot, axis=-1)
    is_real = route_entries < EXPERTS
    destination = jnp.where(
        is_real,
        route_entries * slot_count
        + jnp.arange(seq_count, dtype=jnp.int32)[:, None] * CAP
        + slot_rank,
        EXPERTS * slot_count,
    ).reshape(-1)
    entry_rows = jnp.repeat(normalized_narrow.reshape(-1, model_width), 2, axis=0)
    send_rows = (
        jnp.zeros((EXPERTS * slot_count + 1, model_width), jnp.bfloat16)
        .at[destination]
        .set(entry_rows)[:-1]
        .reshape(EXPERTS, 1, slot_count, model_width)
    )
    received = lax.all_to_all(send_rows, "expert", split_axis=0, concat_axis=1, tiled=True)
    gate_pre = jnp.einsum("ensi,eif->ensf", received, gate_full, preferred_element_type=jnp.float32)
    up_pre = jnp.einsum("ensi,eif->ensf", received, up_full, preferred_element_type=jnp.float32)
    hidden = (jax.nn.silu(gate_pre) * up_pre).astype(jnp.bfloat16)
    result = jnp.einsum(
        "ensf,efi->ensi", hidden, down_full, preferred_element_type=jnp.float32
    ).astype(jnp.bfloat16)
    returned = lax.all_to_all(result, "expert", split_axis=1, concat_axis=0, tiled=True)
    zero_row = jnp.zeros((1, model_width), jnp.bfloat16)
    expert_vals = jnp.concatenate([returned.reshape(-1, model_width), zero_row], axis=0)[
        destination
    ].astype(jnp.float32)
    flat_routes = routes.reshape(-1)
    copy_rows = jnp.repeat(normed_two.reshape(-1, model_width), 2, axis=0)
    const_wide = const_full.astype(jnp.float32)
    is_copy = (flat_routes == EXPERTS + 1)[:, None]
    first_const = (flat_routes == EXPERTS + 2).astype(jnp.float32)[:, None]
    second_const = (flat_routes == EXPERTS + 3).astype(jnp.float32)[:, None]
    entry_vals = (
        expert_vals
        + jnp.where(is_copy, copy_rows, 0.0)
        + first_const * const_wide[:, 0][None, :]
        + second_const * const_wide[:, 1][None, :]
    )
    entry_vals = entry_vals.reshape(seq_count, pos_count, 2, model_width)
    layer_out = middle + jnp.sum(gate_probs[..., None] * entry_vals, axis=2)
    grad_mixed = out_cotangent.astype(jnp.float32)
    grad_gates = jnp.sum(grad_mixed[:, :, None, :] * entry_vals, axis=-1)
    grad_chosen = gate_probs * (
        grad_gates - jnp.sum(gate_probs * grad_gates, axis=-1, keepdims=True)
    )
    choice_ids = jnp.arange(EXPERTS + 4, dtype=jnp.int32)
    prior_logits_gradient = jnp.sum(
        (routes[..., None] == choice_ids).astype(jnp.float32) * grad_chosen[..., None], axis=2
    )
    grad_entries = (gate_probs[..., None] * grad_mixed[:, :, None, :]).reshape(-1, model_width)
    send_grads = (
        jnp.zeros((EXPERTS * slot_count + 1, model_width), jnp.bfloat16)
        .at[destination]
        .set(grad_entries.astype(jnp.bfloat16))[:-1]
        .reshape(EXPERTS, 1, slot_count, model_width)
    )
    owner_grads = lax.all_to_all(send_grads, "expert", split_axis=0, concat_axis=1, tiled=True)
    sigmoid_gate = jax.nn.sigmoid(gate_pre)
    silu_gate = gate_pre * sigmoid_gate
    hidden_back = (silu_gate * up_pre).astype(jnp.bfloat16)
    grad_hidden = jnp.einsum(
        "ensd,efd->ensf", owner_grads, down_full, preferred_element_type=jnp.float32
    )
    grad_gate_pre = (
        grad_hidden * up_pre * sigmoid_gate * (1.0 + gate_pre * (1.0 - sigmoid_gate))
    ).astype(jnp.bfloat16)
    grad_up_pre = (grad_hidden * silu_gate).astype(jnp.bfloat16)
    down_part = jnp.einsum(
        "ensf,ensd->efd", hidden_back, owner_grads, preferred_element_type=jnp.float32
    )
    gate_part = jnp.einsum(
        "ensi,ensf->eif", received, grad_gate_pre, preferred_element_type=jnp.float32
    )
    up_part = jnp.einsum(
        "ensi,ensf->eif", received, grad_up_pre, preferred_element_type=jnp.float32
    )
    grad_rows = (
        jnp.einsum("ensf,eif->ensi", grad_gate_pre, gate_full, preferred_element_type=jnp.float32)
        + jnp.einsum("ensf,eif->ensi", grad_up_pre, up_full, preferred_element_type=jnp.float32)
    ).astype(jnp.bfloat16)
    rows_back = lax.all_to_all(grad_rows, "expert", split_axis=1, concat_axis=0, tiled=True)
    gate_grad, up_grad, down_grad = (
        lax.psum_scatter(
            gate_part.astype(jnp.bfloat16), "shard", scatter_dimension=1, tiled=True
        ).astype(jnp.float32),
        lax.psum_scatter(
            up_part.astype(jnp.bfloat16), "shard", scatter_dimension=1, tiled=True
        ).astype(jnp.float32),
        lax.psum_scatter(
            down_part.astype(jnp.bfloat16), "shard", scatter_dimension=1, tiled=True
        ).astype(jnp.float32),
    )
    grad_row_entries = jnp.concatenate([rows_back.reshape(-1, model_width), zero_row], axis=0)[
        destination
    ].astype(jnp.float32)
    grad_copy = jnp.where(is_copy, grad_entries, 0.0)
    router_widened = router_weight_wide.astype(jnp.float32)
    grad_normed_two = jnp.sum(
        (grad_row_entries + grad_copy).reshape(seq_count, pos_count, 2, model_width), axis=2
    ) + jnp.einsum(
        "hwk,ok->hwo", prior_logits_gradient, router_widened, precision=lax.Precision.HIGHEST
    )
    router_part = jnp.einsum(
        "vrx,vrb->xb",
        normalized_narrow.astype(jnp.float32),
        prior_logits_gradient,
        precision=lax.Precision.HIGHEST,
    )
    const_part = jnp.stack(
        [jnp.sum(first_const * grad_entries, axis=0), jnp.sum(second_const * grad_entries, axis=0)],
        axis=-1,
    )
    moe_gain_part = jnp.sum(grad_normed_two * scaled_two, axis=(0, 1))
    grad_middle = grad_mixed + rms_back(grad_normed_two * moe_gain_wide, middle, inverse_two)
    gradient_projected = grad_middle.astype(jnp.bfloat16)
    output_part = jnp.einsum(
        "vrx,vrb->xb",
        attention_output_narrow,
        gradient_projected,
        preferred_element_type=jnp.float32,
    )
    grad_attended = jnp.einsum(
        "hwk,ok->hwo", gradient_projected, output_weight_wide, preferred_element_type=jnp.float32
    ).astype(jnp.bfloat16)
    delta_rows = jnp.sum(
        (grad_attended.astype(jnp.float32) * attention_output).reshape(
            seq_count, pos_count, HEADS, -1
        ),
        axis=-1,
    )
    delta_sum = jnp.transpose(delta_rows, (0, 2, 1))

    def backward_one(packed):
        return attend_backward(
            packed[0],
            packed[1],
            packed[2],
            packed[3],
            packed[4],
            packed[5],
            packed[6],
            offset,
            block_count,
            width_block,
        )

    grad_query_rot, grad_keys_all, grad_values_all = lax.map(
        backward_one,
        (query_rot, keys_all, values_all, segment_ids, log_total, delta_sum, grad_attended),
    )
    grad_keys, grad_values = (
        lax.psum_scatter(
            grad_keys_all.astype(jnp.bfloat16), "expert", scatter_dimension=1, tiled=True
        ).astype(jnp.float32),
        lax.psum_scatter(
            grad_values_all.astype(jnp.bfloat16), "expert", scatter_dimension=1, tiled=True
        ).astype(jnp.float32),
    )
    gradient_query_unrotated = rotary(grad_query_rot, positions, -1.0).astype(jnp.bfloat16)
    gradient_key_unrotated = rotary(grad_keys, positions, -1.0).astype(jnp.bfloat16)
    gradient_value_narrow = grad_values.astype(jnp.bfloat16)
    query_part = jnp.einsum(
        "vrx,vrb->xb",
        normalized_first,
        gradient_query_unrotated,
        preferred_element_type=jnp.float32,
    )
    key_part = jnp.einsum(
        "vrx,vrb->xb", normalized_first, gradient_key_unrotated, preferred_element_type=jnp.float32
    )
    value_part = jnp.einsum(
        "vrx,vrb->xb", normalized_first, gradient_value_narrow, preferred_element_type=jnp.float32
    )
    grad_normed_one = jnp.einsum(
        "hwk,ok->hwo",
        gradient_query_unrotated,
        query_weight_wide,
        preferred_element_type=jnp.float32,
    )
    grad_normed_one = grad_normed_one + jnp.einsum(
        "hwk,ok->hwo", gradient_key_unrotated, key_weight_wide, preferred_element_type=jnp.float32
    )
    grad_normed_one = grad_normed_one + jnp.einsum(
        "hwk,ok->hwo", gradient_value_narrow, value_weight_wide, preferred_element_type=jnp.float32
    )
    attn_gain_part = jnp.sum(grad_normed_one * scaled_one, axis=(0, 1))
    tokens_grad = grad_middle + rms_back(grad_normed_one * attn_gain_wide, tokens_wide, inverse_one)
    layer_parts = (
        lax.psum_scatter(
            query_part.astype(jnp.bfloat16), "shard", scatter_dimension=0, tiled=True
        ).astype(jnp.float32),
        lax.psum_scatter(
            key_part.astype(jnp.bfloat16), "shard", scatter_dimension=0, tiled=True
        ).astype(jnp.float32),
        lax.psum_scatter(
            value_part.astype(jnp.bfloat16), "shard", scatter_dimension=0, tiled=True
        ).astype(jnp.float32),
        lax.psum_scatter(
            output_part.astype(jnp.bfloat16), "shard", scatter_dimension=0, tiled=True
        ).astype(jnp.float32),
        lax.psum_scatter(
            router_part.astype(jnp.bfloat16), "shard", scatter_dimension=0, tiled=True
        ).astype(jnp.float32),
        lax.psum_scatter(
            const_part.astype(jnp.bfloat16), "shard", scatter_dimension=0, tiled=True
        ).astype(jnp.float32),
        lax.psum_scatter(
            attn_gain_part.astype(jnp.bfloat16), "shard", scatter_dimension=0, tiled=True
        ).astype(jnp.float32),
        lax.psum_scatter(
            moe_gain_part.astype(jnp.bfloat16), "shard", scatter_dimension=0, tiled=True
        ).astype(jnp.float32),
    )
    layer_grads = (
        lax.psum(layer_parts[0].astype(jnp.bfloat16), "expert").astype(jnp.float32),
        lax.psum(layer_parts[1].astype(jnp.bfloat16), "expert").astype(jnp.float32),
        lax.psum(layer_parts[2].astype(jnp.bfloat16), "expert").astype(jnp.float32),
        lax.psum(layer_parts[3].astype(jnp.bfloat16), "expert").astype(jnp.float32),
        lax.psum(layer_parts[4].astype(jnp.bfloat16), "expert").astype(jnp.float32),
        lax.psum(layer_parts[5].astype(jnp.bfloat16), "expert").astype(jnp.float32),
        lax.psum(layer_parts[6].astype(jnp.bfloat16), "expert").astype(jnp.float32),
        lax.psum(layer_parts[7].astype(jnp.bfloat16), "expert").astype(jnp.float32),
    )
    return (
        layer_out.astype(jnp.bfloat16),
        tokens_grad,
        prior_logits_gradient,
        layer_grads[0],
        layer_grads[1],
        layer_grads[2],
        layer_grads[3],
        layer_grads[4],
        layer_grads[5],
        layer_grads[6],
        layer_grads[7],
        gate_grad,
        up_grad,
        down_grad,
    )


RING = 4
PAIR = 2
LOCAL = 4
META = 16


def z_pairs(step):
    lines = PAIR * PAIR
    return [
        (z * lines + rest, (z + step) % RING * lines + rest)
        for z in range(RING)
        for rest in range(lines)
    ]


def along_z(values, step):
    return lax.ppermute(values, "shard", z_pairs(step))


def across_y(values):
    return lax.ppermute(values, "shard", [(s, s ^ PAIR) for s in range(RING * PAIR * PAIR)])


def across_core(values):
    return lax.ppermute(values, "shard", [(s, s ^ 1) for s in range(RING * PAIR * PAIR)])


def across_x(values):
    return lax.ppermute(values, "expert", [(0, 1), (1, 0)])


def together(*values):
    return lax.optimization_barrier(values)


def gather_rows(own, beside=()):
    ring, crossed = [own], []
    for step in range(RING - 1):
        following, other = along_z(ring[-1], 1), across_x(ring[-1])
        if step == 1 and beside:
            following, other, beside = together(following, other, beside)
        else:
            following, other = together(following, other)
        ring.append(following)
        crossed.append(other)
    return ring + crossed + [across_x(ring[-1])], beside


def add_all(*values):
    return sum(value.astype(jnp.float32) for value in values)


def reduce_rows(parts, beside, late):
    other, beside = together(across_x(parts[2 * RING - 1]), beside)
    total = add_all(parts[RING - 1], other)
    for step in reversed(range(RING - 1)):
        passed, other = along_z(total.astype(jnp.bfloat16), -1), across_x(parts[RING + step])
        if step == 1:
            passed, other, late = together(passed, other, late)
        else:
            passed, other = together(passed, other)
        total = add_all(parts[step], passed, other)
    return total, beside, late


def plane_groups():
    lines = PAIR * PAIR
    return [[z * lines + i for i in range(lines)] for z in range(RING)]


def scatter_plane(part):
    return lax.psum_scatter(
        part, "shard", scatter_dimension=0, axis_index_groups=plane_groups(), tiled=False
    )


def gather_plane(part):
    return lax.all_gather(part, "shard", axis=0, axis_index_groups=plane_groups(), tiled=False)


def split_core(part, core_place):
    rows, width = part.shape
    part = part.reshape(RING, PAIR, PAIR, rows // (RING * PAIR * PAIR), width)
    mine = jnp.where(core_place == 0, part[:, :, 0], part[:, :, 1])
    other = jnp.where(core_place == 0, part[:, :, 1], part[:, :, 0])
    return mine, other


def reduce_packed(parts, z_place, y_place, first_grad, late):
    total = None
    for step in reversed(range(RING)):
        owner = lax.rem(z_place - step + RING, RING)
        blocks = [lax.dynamic_index_in_dim(part, owner, 0, keepdims=False) for part in parts]
        block = jnp.concatenate(blocks, axis=-1)
        other = across_y(jnp.where(y_place == 0, block[1], block[0]))
        mine = jnp.where(y_place == 0, block[0], block[1])
        if total is None:
            other, first_grad = together(other, first_grad)
            here = add_all(mine, other)
            shared = lax.ppermute(first_grad, "expert", [(1, 0)])
        else:
            passed, other = together(along_z(total, -1), other)
            if step == 1:
                passed, shared, late = together(passed, shared, late)
            here = add_all(mine, passed, other)
        total = here.astype(jnp.bfloat16)
    return add_all(total, across_x(total)), shared, late


def meta_rows(rows, width):
    filled = jnp.concatenate(rows, axis=-1).reshape(len(rows) // 2, -1)
    return jnp.pad(filled, ((0, META - filled.shape[0]), (0, width - filled.shape[1]))).astype(
        jnp.bfloat16
    )


def dot_rows(left, right):
    return lax.dot_general(left, right, (((1,), (0,)), ((), ())), preferred_element_type=jnp.float32)


def dot_wide(left, right):
    return lax.dot_general(left, right, (((1,), (1,)), ((), ())), preferred_element_type=jnp.float32)


def dot_tall(left, right):
    return lax.dot_general(left, right, (((0,), (0,)), ((), ())), preferred_element_type=jnp.float32)


def pick_kernel(place, *refs):
    block_count = RING * PAIR
    grads = refs[:block_count]
    pick_ref, slot_ref = refs[block_count:]
    rows = pick_ref.shape[2]
    later = lax.broadcasted_iota(jnp.int32, (rows, rows), 1)
    earlier = lax.broadcasted_iota(jnp.int32, (rows, rows), 0)
    before = jnp.where(earlier < later, 1.0, 0.0).astype(jnp.bfloat16)
    wanted = (lax.broadcasted_iota(jnp.int32, (8, rows), 0) + place[0] * LOCAL).astype(
        jnp.float32
    )
    inside = lax.broadcasted_iota(jnp.int32, (8, rows), 0) < LOCAL
    ranks = lax.broadcasted_iota(jnp.int32, (CAP, rows), 0).astype(jnp.float32)
    for block in range(block_count):
        meta = grads[block][rows : rows + META, :].astype(jnp.float32)
        first = meta[1:2, :rows]
        second = meta[1:2, rows : 2 * rows]
        named = jnp.where(((first == wanted) | (second == wanted)) & inside, 1.0, 0.0)
        rank = dot_rows(named.astype(jnp.bfloat16), before)
        pieces = []
        for expert in range(LOCAL):
            hit = (rank[expert : expert + 1] == ranks) & (named[expert : expert + 1] > 0.5)
            pieces.append(jnp.where(hit, 1.0, 0.0))
        pick = jnp.concatenate(pieces, axis=0).astype(jnp.bfloat16)
        pick_ref[block] = pick
        slot_ref[block] = dot_rows(pick, grads[block][:rows, :]).astype(jnp.bfloat16)


def prepare_kernel(place, slot_ref, own_ref, moved_ref, *refs):
    downs = refs[:4]
    back_ref, wide_ref, down_ref = refs[4:]
    number = pl.program_id(0)
    block_count = slot_ref.shape[0]
    half = wide_ref.shape[2] // 2
    depth = own_ref.shape[3]
    for line in range(PAIR * PAIR):
        for step in range(RING):
            owner = lax.rem(place[1] - step + RING, RING) * (PAIR * PAIR) + line
            start = pl.multiple_of(owner * depth, 16)
            for side in range(2):
                piece = own_ref[line, side, 0] if step == 0 else moved_ref[line, step - 1, side, 0]
                wide_ref[0, pl.ds(start, depth), side * half : (side + 1) * half] = piece
        part = downs[line]
        deep = part.shape[1]
        source = (place[2] ^ (line % PAIR)) * PAIR + (place[3] ^ (line // PAIR))
        down_ref[0, pl.ds(pl.multiple_of(source * deep, 16), deep), :] = part[0]
    width = slot_ref.shape[2]
    mine = slot_ref[:, pl.ds(pl.multiple_of(number * CAP, CAP), CAP), :]
    back_ref[0] = dot_wide(mine.reshape(block_count * CAP, width), down_ref[0])


def expert_kernel(place, *refs):
    block_count = RING * PAIR
    tokens = refs[:block_count]
    pick_ref, wide_ref, down_ref, back_ref = refs[block_count : block_count + 4]
    rest = refs[block_count + 4 :]
    slot_ref, hidden_ref, mixed_ref = rest[:3]
    grad_refs = rest[3 : 3 + block_count]
    out_refs = rest[3 + block_count : 3 + 2 * block_count]
    out_slots, grad_slots, gate_grads = rest[3 + 2 * block_count :]
    number = pl.program_id(0)
    rows = pick_ref.shape[2]
    width = slot_ref.shape[2]
    half = wide_ref.shape[2] // 2

    @pl.when(number == 0)
    def _():
        gate_grads[...] = jnp.zeros_like(gate_grads)
        for block in range(block_count):
            slot_ref[block] = dot_rows(pick_ref[block], tokens[block][:rows, :]).astype(
                jnp.bfloat16
            )

    span = pl.ds(pl.multiple_of(number * CAP, CAP), CAP)
    mine = slot_ref[:, span, :].reshape(block_count * CAP, width)
    both = dot_rows(mine, wide_ref[0])
    gate = both[:, :half]
    up = both[:, half:]
    sigmoid = 1.0 / (1.0 + jnp.exp(-gate))
    silu = gate * sigmoid
    hidden = silu * up
    back = back_ref[0]
    expert_id = (number + place[0] * LOCAL).astype(jnp.float32)
    chances = []
    product = jnp.sum(hidden * back, axis=1, keepdims=True)
    for block in range(block_count):
        meta = tokens[block][rows : rows + META, :].astype(jnp.float32)
        first = jnp.where(meta[1:2, :rows] == expert_id, 1.0, 0.0)
        second = jnp.where(meta[1:2, rows : 2 * rows] == expert_id, 1.0, 0.0)
        pick = pick_ref[block, span, :].astype(jnp.float32)
        chance = first * meta[0:1, :rows] + second * meta[0:1, rows : 2 * rows]
        chances.append(jnp.sum(pick * chance, axis=1, keepdims=True))
        spread = jnp.sum(
            pick * product[block * CAP : (block + 1) * CAP], axis=0, keepdims=True
        )
        gate_grads[block, 0:1, :rows] += first * spread
        gate_grads[block, 0:1, rows : 2 * rows] += second * spread
    chance = jnp.concatenate(chances, axis=0)
    back = back * chance
    weighted = (hidden * chance).astype(jnp.bfloat16)
    grad_gate = back * up * sigmoid * (1.0 + gate * (1.0 - sigmoid))
    grad_up = back * silu
    mixed = jnp.concatenate([grad_gate, grad_up], axis=1).astype(jnp.bfloat16)
    hidden_ref[0] = weighted
    mixed_ref[0] = mixed
    out_part = dot_rows(weighted, down_ref[0]).astype(jnp.bfloat16)
    out_slots[:, span, :] = out_part.reshape(block_count, CAP, width)
    grad_part = dot_wide(mixed, wide_ref[0]).astype(jnp.bfloat16)
    grad_slots[:, span, :] = grad_part.reshape(block_count, CAP, width)

    @pl.when(number == LOCAL - 1)
    def _():
        for block in range(block_count):
            pick = pick_ref[block]
            grad_refs[block][:rows, :] = dot_tall(pick, grad_slots[block]).astype(jnp.bfloat16)
            grad_refs[block][rows : rows + META, :] = gate_grads[block].astype(jnp.bfloat16)
            out_refs[block][...] = dot_tall(pick, out_slots[block]).astype(jnp.bfloat16)


def weight_grad_kernel(place, *refs):
    slot_ref, back_ref, hidden_ref, mixed_ref, wide_ref, down_ref, wide_sum = refs
    number = pl.program_id(0)
    block_count, _, width = slot_ref.shape
    span = pl.ds(pl.multiple_of(number * CAP, CAP), CAP)
    rows = slot_ref[:, span, :].reshape(block_count * CAP, width)
    wide_sum[...] = dot_tall(rows, mixed_ref[0])
    grads = back_ref[:, span, :].reshape(block_count * CAP, width)
    half = wide_sum.shape[1] // 2
    deep = down_ref.shape[2]
    depth = wide_ref.shape[4]
    for line in range(PAIR * PAIR):
        for step in range(RING):
            owner = lax.rem(place[1] - step + RING, RING) * (PAIR * PAIR) + line
            part = wide_sum[pl.ds(pl.multiple_of(owner * depth, 16), depth), :]
            wide_ref[line, step, 0, 0] = part[:, :half].astype(jnp.bfloat16)
            wide_ref[line, step, 1, 0] = part[:, half:].astype(jnp.bfloat16)
        columns = hidden_ref[0, :, line * deep : (line + 1) * deep]
        down_ref[line, 0] = dot_tall(columns, grads).astype(jnp.bfloat16)


def busy(microseconds):
    return pl.CostEstimate(
        flops=microseconds * 400_000_000,
        transcendentals=0,
        bytes_accessed=microseconds * 3_000_000,
    )


def whole(shape):
    return pl.BlockSpec(shape, lambda number, place: (0,) * len(shape))


def by_expert(shape, axis=0):
    return pl.BlockSpec(
        shape,
        lambda number, place: tuple(number if d == axis else 0 for d in range(len(shape))),
    )


def pick_slots(place, grads):
    padded, width = grads[0].shape
    rows = padded - META
    blocks = len(grads)
    shapes = [(blocks, LOCAL * CAP, rows), (blocks, LOCAL * CAP, width)]
    return pl.pallas_call(
        pick_kernel,
        name="pick_slots",
        cost_estimate=busy(4),
        out_shape=[jax.ShapeDtypeStruct(shape, jnp.bfloat16) for shape in shapes],
        grid_spec=pltpu.PrefetchScalarGridSpec(
            num_scalar_prefetch=1,
            grid=(1,),
            in_specs=[whole(g.shape) for g in grads],
            out_specs=[whole(shape) for shape in shapes],
        ),
    )(place, *grads)


def prepare_experts(place, slot_rows, own, moved, downs):
    blocks, _, width = slot_rows.shape
    lines, _, local, depth, span = own.shape
    deep = downs[0].shape[1]
    model = depth * RING * lines
    slots = blocks * CAP
    shapes = [
        ((local, slots, span), jnp.float32),
        ((local, model, 2 * span), jnp.bfloat16),
        ((local, deep * lines, width), jnp.bfloat16),
    ]
    return pl.pallas_call(
        prepare_kernel,
        name="prepare_experts",
        cost_estimate=busy(10),
        out_shape=[jax.ShapeDtypeStruct(s, d) for s, d in shapes],
        grid_spec=pltpu.PrefetchScalarGridSpec(
            num_scalar_prefetch=1,
            grid=(local,),
            in_specs=[
                whole(slot_rows.shape),
                by_expert((lines, 2, 1, depth, span), 2),
                by_expert((lines, RING - 1, 2, 1, depth, span), 3),
            ]
            + [by_expert((1, deep, width))] * 4,
            out_specs=[
                by_expert((1, slots, span)),
                by_expert((1, model, 2 * span)),
                by_expert((1, deep * lines, width)),
            ],
        ),
    )(place, slot_rows, own, moved, *downs)


def run_experts(place, tokens, pick, wide, down, back):
    padded, width = tokens[0].shape
    rows = padded - META
    blocks = len(tokens)
    local, model, span2 = wide.shape
    span = span2 // 2
    slots = blocks * CAP
    shapes = [
        ((blocks, local * CAP, width), jnp.bfloat16),
        ((local, slots, span), jnp.bfloat16),
        ((local, slots, span2), jnp.bfloat16),
    ]
    shapes = shapes + [((padded, width), jnp.bfloat16)] * blocks
    shapes = shapes + [((rows, width), jnp.bfloat16)] * blocks
    results = pl.pallas_call(
        expert_kernel,
        name="run_experts",
        cost_estimate=busy(22),
        out_shape=[jax.ShapeDtypeStruct(s, d) for s, d in shapes],
        grid_spec=pltpu.PrefetchScalarGridSpec(
            num_scalar_prefetch=1,
            grid=(local,),
            in_specs=[whole(t.shape) for t in tokens]
            + [
                whole(pick.shape),
                by_expert((1, model, span2)),
                by_expert((1, span, width)),
                by_expert((1, slots, span)),
            ],
            out_specs=[
                whole(shapes[0][0]),
                by_expert((1, slots, span)),
                by_expert((1, slots, span2)),
            ]
            + [whole(s) for s, _ in shapes[3:]],
            scratch_shapes=[
                pltpu.VMEM((blocks, local * CAP, width), jnp.bfloat16),
                pltpu.VMEM((blocks, local * CAP, width), jnp.bfloat16),
                pltpu.VMEM((blocks, META, width), jnp.float32),
            ],
        ),
    )(place, *tokens, pick, wide, down, back)
    return results[:3], results[3 : 3 + blocks], results[3 + blocks :]


def weight_grads(place, slots, backs, hidden, mixed):
    blocks, total, width = slots.shape
    local, rows, span = hidden.shape
    lines = PAIR * PAIR
    depth = width // (RING * lines)
    deep = span // lines
    return pl.pallas_call(
        weight_grad_kernel,
        name="weight_grads",
        cost_estimate=busy(12),
        out_shape=[
            jax.ShapeDtypeStruct((lines, RING, 2, local, depth, span), jnp.bfloat16),
            jax.ShapeDtypeStruct((lines, local, deep, width), jnp.bfloat16),
        ],
        grid_spec=pltpu.PrefetchScalarGridSpec(
            num_scalar_prefetch=1,
            grid=(local,),
            in_specs=[
                whole(slots.shape),
                whole(backs.shape),
                by_expert((1, rows, span)),
                by_expert((1, rows, 2 * span)),
            ],
            out_specs=[
                by_expert((lines, RING, 2, 1, depth, span), 3),
                by_expert((lines, 1, deep, width), 1),
            ],
            scratch_shapes=[pltpu.VMEM((width, 2 * span), jnp.float32)],
        ),
    )(place, slots, backs, hidden, mixed)


def add_low(left, right):
    return (left.astype(jnp.float32) + right.astype(jnp.float32)).astype(jnp.bfloat16)


def turn_pairs(values, cosine, sine):
    half = values.shape[1] // 4
    lane = lax.rem(lax.broadcasted_iota(jnp.int32, values.shape, 1), 2 * half)
    swapped = jnp.where(
        lane < half,
        pltpu.roll(values, 3 * half, 1),
        pltpu.roll(values, half, 1),
    )
    return values * cosine + swapped * sine


def mask_bias(x_place, rows, columns, row_segments, column_segments):
    row = lax.broadcasted_iota(jnp.int32, (rows, columns), 0) + x_place * rows
    column = lax.broadcasted_iota(jnp.int32, (rows, columns), 1)
    return jnp.where((column <= row) & (row_segments == column_segments), 0.0, masked_fill)


def attention_forward_kernel(
    place,
    normed_ref,
    query_weight,
    key_weight,
    value_weight,
    output_weight,
    cosine_ref,
    sine_ref,
    column_ref,
    row_ref,
    query_ref,
    key_ref,
    value_ref,
    mixed_ref,
    total_ref,
    result_ref,
    bias_ref,
):
    rows, columns = bias_ref.shape
    own = pl.ds(pl.multiple_of(place[0] * rows, rows), rows)

    @pl.when(pl.program_id(0) == 0)
    def _():
        bias_ref[...] = mask_bias(place[0], rows, columns, column_ref[own, :], row_ref[...])
        result_ref[...] = jnp.zeros_like(result_ref)

    normed = normed_ref[...]
    query = dot_rows(normed_ref[own, :], query_weight[...])
    query = turn_pairs(query, cosine_ref[own, :], sine_ref[own, :]).astype(jnp.bfloat16)
    key = turn_pairs(dot_rows(normed, key_weight[...]), cosine_ref[...], sine_ref[...])
    key = key.astype(jnp.bfloat16)
    value = dot_rows(normed, value_weight[...]).astype(jnp.bfloat16)
    query_ref[...] = query
    key_ref[...] = key
    value_ref[...] = value
    width = query.shape[1]
    low = lax.broadcasted_iota(jnp.int32, (rows, width), 1) < width // 2
    scale = (width // 2) ** (-0.5)
    sides = []
    for side in range(2):
        keep = low if side == 0 else jnp.logical_not(low)
        scores = dot_wide(jnp.where(keep, query, 0), key) * scale + bias_ref[...]
        top = jnp.max(scores, axis=1, keepdims=True)
        terms = jnp.exp(scores - top)
        count = jnp.sum(terms, axis=1, keepdims=True)
        probs = (terms * (1.0 / count)).astype(jnp.bfloat16)
        sides.append((dot_rows(probs, value), top + jnp.log(count)))
    mixed = jnp.where(low, sides[0][0], sides[1][0])
    mixed_ref[...] = mixed
    total_ref[0] = jnp.where(low, sides[0][1], sides[1][1])
    result_ref[...] += dot_rows(mixed.astype(jnp.bfloat16), output_weight[...])


def attention_backward_kernel(
    place,
    normed_ref,
    query_weight,
    key_weight,
    value_weight,
    output_weight,
    cosine_ref,
    sine_ref,
    column_ref,
    row_ref,
    query_ref,
    key_ref,
    value_ref,
    mixed_ref,
    total_ref,
    grad_ref,
    weight_mine,
    weight_other,
    result_ref,
    bias_ref,
    weight_ref,
):
    rows, columns = bias_ref.shape
    own = pl.ds(pl.multiple_of(place[0] * rows, rows), rows)

    @pl.when(pl.program_id(0) == 0)
    def _():
        bias_ref[...] = mask_bias(place[0], rows, columns, column_ref[own, :], row_ref[...])
        result_ref[...] = jnp.zeros_like(result_ref)

    normed = normed_ref[...]
    grad = grad_ref[...]
    query, key, value, mixed = query_ref[...], key_ref[...], value_ref[...], mixed_ref[...]
    attended = dot_wide(grad, output_weight[...]).astype(jnp.bfloat16)
    product = attended.astype(jnp.float32) * mixed
    width = query.shape[1]
    low = lax.broadcasted_iota(jnp.int32, (rows, width), 1) < width // 2
    low_keys = lax.broadcasted_iota(jnp.int32, (columns, width), 1) < width // 2
    scale = (width // 2) ** (-0.5)
    sides = []
    for side in range(2):
        keep = low if side == 0 else jnp.logical_not(low)
        start = side * (width // 2)
        delta = jnp.sum(jnp.where(keep, product, 0.0), axis=1, keepdims=True)
        scores = dot_wide(jnp.where(keep, query, 0), key) * scale + bias_ref[...]
        probs = jnp.exp(scores - total_ref[0, :, start : start + 1])
        grad_probs = dot_wide(jnp.where(keep, attended, 0), value)
        grad_scores = (probs * (grad_probs - delta) * scale).astype(jnp.bfloat16)
        sides.append(
            (
                dot_rows(grad_scores, key),
                dot_tall(grad_scores, query),
                dot_tall(probs.astype(jnp.bfloat16), attended),
            )
        )
    grad_query = jnp.where(low, sides[0][0], sides[1][0])
    grad_key = jnp.where(low_keys, sides[0][1], sides[1][1])
    grad_value = jnp.where(low_keys, sides[0][2], sides[1][2]).astype(jnp.bfloat16)
    grad_query = turn_pairs(grad_query, cosine_ref[own, :], -sine_ref[own, :])
    grad_query = grad_query.astype(jnp.bfloat16)
    grad_key = turn_pairs(grad_key, cosine_ref[...], -sine_ref[...]).astype(jnp.bfloat16)
    result_ref[...] += dot_wide(grad_key, key_weight[...]) + dot_wide(
        grad_value, value_weight[...]
    )
    result_ref[own, :] += dot_wide(grad_query, query_weight[...])
    weight_ref[:, :width] = dot_tall(normed_ref[own, :], grad_query)
    weight_ref[:, width : 2 * width] = dot_tall(normed, grad_key)
    weight_ref[:, 2 * width :] = dot_tall(normed, grad_value)
    depth = weight_mine.shape[3]
    for z in range(RING):
        for y in range(PAIR):
            pair = (z * PAIR + y) * PAIR
            near = pl.ds(pl.multiple_of((pair + place[3]) * depth, 16), depth)
            far = pl.ds(pl.multiple_of((pair + 1 - place[3]) * depth, 16), depth)
            for kind in range(3):
                span = slice(kind * width, (kind + 1) * width)
                weight_mine[kind, z, y] = weight_ref[near, span].astype(jnp.bfloat16)
                weight_other[kind, z, y] = weight_ref[far, span].astype(jnp.bfloat16)


def attention_specs(normed, weights, cosine, column, row, first):
    columns, model = normed.shape
    pairs = HEADS // 2
    width = model // pairs

    def block(shape, index):
        return pl.BlockSpec(shape, lambda number, place: index(number + first))

    return [
        whole(normed.shape),
        block((model, width), lambda n: (0, n)),
        block((model, width), lambda n: (0, pairs + n)),
        block((model, width), lambda n: (0, 2 * pairs + n)),
        block((width, model), lambda n: (n, 3)),
        whole(cosine.shape),
        whole(cosine.shape),
        whole(column.shape),
        whole(row.shape),
    ]


def attention_forward(place, normed, weights, cosine, sine, column, row):
    columns, model = normed.shape
    rows = columns // PAIR
    pairs = HEADS // 2
    width = model // pairs
    across = lambda size: pl.BlockSpec((size, width), lambda number, place: (0, number))
    return pl.pallas_call(
        attention_forward_kernel,
        name="attention_forward",
        cost_estimate=busy(15),
        out_shape=[
            jax.ShapeDtypeStruct((rows, model), jnp.bfloat16),
            jax.ShapeDtypeStruct((columns, model), jnp.bfloat16),
            jax.ShapeDtypeStruct((columns, model), jnp.bfloat16),
            jax.ShapeDtypeStruct((rows, model), jnp.float32),
            jax.ShapeDtypeStruct((pairs, rows, width), jnp.float32),
            jax.ShapeDtypeStruct((rows, model), jnp.float32),
        ],
        grid_spec=pltpu.PrefetchScalarGridSpec(
            num_scalar_prefetch=1,
            grid=(pairs,),
            in_specs=attention_specs(normed, weights, cosine, column, row, 0),
            out_specs=[
                across(rows),
                across(columns),
                across(columns),
                across(rows),
                by_expert((1, rows, width)),
                whole((rows, model)),
            ],
            scratch_shapes=[pltpu.VMEM((rows, columns), jnp.float32)],
        ),
    )(place, normed, weights, weights, weights, weights, cosine, sine, column, row)


def attention_backward(place, normed, weights, cosine, sine, column, row, kept, grad, first, count):
    columns, model = normed.shape
    rows = columns // PAIR
    width = model // (HEADS // 2)
    depth = model // (RING * PAIR * PAIR)
    across = lambda size: pl.BlockSpec((size, width), lambda number, place: (0, number + first))
    return pl.pallas_call(
        attention_backward_kernel,
        name="attention_backward",
        cost_estimate=busy(9),
        out_shape=[
            jax.ShapeDtypeStruct((3, RING, PAIR, depth, width * count), jnp.bfloat16),
            jax.ShapeDtypeStruct((3, RING, PAIR, depth, width * count), jnp.bfloat16),
            jax.ShapeDtypeStruct((columns, model), jnp.float32),
        ],
        grid_spec=pltpu.PrefetchScalarGridSpec(
            num_scalar_prefetch=1,
            grid=(count,),
            in_specs=attention_specs(normed, weights, cosine, column, row, first)
            + [
                across(rows),
                across(columns),
                across(columns),
                across(rows),
                pl.BlockSpec((1, rows, width), lambda number, place: (number + first, 0, 0)),
                whole(grad.shape),
            ],
            out_specs=[
                pl.BlockSpec((3, RING, PAIR, depth, width), lambda n, place: (0, 0, 0, 0, n)),
                pl.BlockSpec((3, RING, PAIR, depth, width), lambda n, place: (0, 0, 0, 0, n)),
                whole((columns, model)),
            ],
            scratch_shapes=[
                pltpu.VMEM((rows, columns), jnp.float32),
                pltpu.VMEM((model, 3 * width), jnp.float32),
            ],
        ),
    )(place, normed, weights, weights, weights, weights, cosine, sine, column, row, *kept, grad)


def weight_pieces(gate_weight, up_weight, z_place):
    span = gate_weight.shape[2] // RING
    pieces = []
    for step in range(RING):
        start = lax.rem(z_place + step, RING) * span
        pieces.append(
            jnp.stack(
                [
                    lax.dynamic_slice_in_dim(gate_weight, start, span, 2),
                    lax.dynamic_slice_in_dim(up_weight, start, span, 2),
                ]
            )
        )
    return pieces


def place_columns(parts, z_place):
    columns = []
    for column in range(RING):
        choice = lax.rem(column - z_place + RING, RING)
        chosen = parts[0]
        for step in range(1, RING):
            chosen = jnp.where(choice == step, parts[step], chosen)
        columns.append(chosen)
    both = jnp.concatenate(columns, axis=-1).astype(jnp.float32)
    return both[0], both[1]


def body_split(
    tokens,
    segment_ids,
    routes,
    earlier_logits,
    out_cotangent,
    query_weight,
    key_weight,
    value_weight,
    output_weight,
    router_weight,
    const_vectors,
    attn_gain,
    moe_gain,
    gate_weight,
    up_weight,
    down_weight,
):
    _, pos_count, model_width = tokens.shape
    tokens, segment_row, routes = tokens[0], segment_ids[0], routes[0]
    earlier_logits, cotangent_low = earlier_logits[0], out_cotangent[0]
    x_place = lax.axis_index("expert")
    shard_place = lax.axis_index("shard")
    z_place = shard_place // (PAIR * PAIR)
    y_place = lax.rem(shard_place // PAIR, PAIR)
    core_place = lax.rem(shard_place, PAIR)
    order = jnp.arange(4, dtype=jnp.int32)
    place = jnp.where(
        order == 0,
        x_place,
        jnp.where(order == 1, z_place, jnp.where(order == 2, y_place, core_place)),
    ).astype(jnp.int32)
    choices = router_weight.shape[1]
    consts = const_vectors.shape[1]
    small_count = choices + consts + 2
    small = jnp.concatenate(
        [router_weight, const_vectors, attn_gain[:, None], moe_gain[:, None]], axis=1
    )
    small = jnp.pad(small, ((0, 0), (0, 128 - small_count)))
    packed = jnp.concatenate(
        [query_weight, key_weight, value_weight, output_weight, small], axis=1
    )
    routes_low = routes.astype(jnp.bfloat16)
    route_rows = [routes_low[:, 0], routes_low[:, 1]]
    zero_rows = [jnp.zeros_like(route_rows[0])] * 2
    cotangent_blocks, _ = gather_rows(
        jnp.concatenate([cotangent_low, meta_rows(zero_rows + route_rows, model_width)], axis=0)
    )
    gathered = lax.all_gather(packed, "shard", axis=0, tiled=True)
    other_tokens = across_x(tokens)
    frequency = jnp.exp(
        (jnp.arange(128, dtype=jnp.int32) % 32).astype(jnp.float32) * (-2.0 * math.log(10000.0) / 64)
    )
    angles = jnp.arange(PAIR * pos_count, dtype=jnp.float32)[:, None] * frequency[None, :]
    cosine = jnp.cos(angles)
    sine = jnp.sin(angles) * jnp.where(jnp.arange(128) % 64 < 32, -1.0, 1.0)
    segment_low = segment_row.astype(jnp.float32)[None, :]
    segment_column = segment_row.astype(jnp.float32)[:, None]
    cosine, sine, gathered, other_tokens, cotangent_blocks = together(
        cosine, sine, gathered, other_tokens, cotangent_blocks
    )
    pieces = weight_pieces(gate_weight, up_weight, z_place)
    down_other = across_y(down_weight)
    moved = [along_z(pieces[1], 1)]
    gathered, other_tokens, cotangent_blocks, pieces, down_other, moved = together(
        gathered, other_tokens, cotangent_blocks, pieces, down_other, moved
    )
    own_wide = gather_plane(pieces[0])
    downs = [down_weight, down_other, across_core(down_weight), across_core(down_other)]
    moved = moved + [along_z(pieces[step], step) for step in range(2, RING)]

    joint = 3 * model_width
    tail = gathered[:, joint + model_width :].astype(jnp.float32)
    router_low = gathered[:, joint + model_width : joint + model_width + choices]
    router_wide = tail[:, :choices]
    const_wide = tail[:, choices : choices + consts].T
    gain_attn = tail[:, choices + consts]
    gain_moe = tail[:, choices + consts + 1]

    first_tokens = jnp.where(x_place == 0, tokens, other_tokens)
    second_tokens = jnp.where(x_place == 0, other_tokens, tokens)
    all_wide = jnp.concatenate([first_tokens, second_tokens], axis=0).astype(jnp.float32)
    scaled_all, _ = rms_parts(all_wide)
    normed_all = (scaled_all * gain_attn).astype(jnp.bfloat16)
    tokens_wide = tokens.astype(jnp.float32)
    _, inverse_one = rms_parts(tokens_wide)
    query_rot, keys_all, values_all, mixed_heads, totals, projected = attention_forward(
        place, normed_all, gathered, cosine, sine, segment_column, segment_low
    )
    projected, moved = together(projected, moved)
    moved_wide = gather_plane(jnp.stack(moved))
    middle = tokens_wide + projected
    scaled_two, inverse_two = rms_parts(middle)
    normed_two = scaled_two * gain_moe
    normed_low = normed_two.astype(jnp.bfloat16)
    router_logits = dot_rows(normed_low, router_low) + earlier_logits
    choice_ids = jnp.arange(choices, dtype=jnp.int32)
    one_hot = (routes[..., None] == choice_ids).astype(jnp.float32)
    chosen = jnp.sum(one_hot * router_logits[:, None, :], axis=-1)
    gate_probs = jax.nn.softmax(chosen, axis=-1)
    probs_low = gate_probs.astype(jnp.bfloat16)
    payload = jnp.concatenate(
        [
            normed_low,
            meta_rows([probs_low[:, 0], probs_low[:, 1]] + route_rows, model_width),
        ],
        axis=0,
    )
    payload, cotangent_blocks = together(payload, cotangent_blocks)
    token_blocks, (pick, back_slots) = gather_rows(
        payload, tuple(pick_slots(place, cotangent_blocks))
    )
    back_hidden, wide_full, down_full = prepare_experts(
        place, back_slots, own_wide, moved_wide, downs
    )
    (token_slots, hidden, mixed), grad_parts, out_parts = run_experts(
        place, token_blocks, pick, wide_full, down_full, back_hidden
    )

    grad_total, (wide_grads, down_grads), out_parts = reduce_rows(
        grad_parts, weight_grads(place, token_slots, back_slots, hidden, mixed), out_parts
    )
    wide_sum = scatter_plane(wide_grads)
    wide_sum, down_grads = together(wide_sum, down_grads)
    down_sum = scatter_plane(down_grads)
    out_other = across_x(out_parts[7])

    cotangent = cotangent_low.astype(jnp.float32)
    copies = jnp.sum(one_hot[..., EXPERTS + 1] * gate_probs, axis=-1)[:, None]
    const_probs = jnp.sum(one_hot[..., EXPERTS + 2 :] * gate_probs[..., None], axis=1)
    copy_dot = jnp.sum(cotangent * normed_two, axis=-1)
    const_dot = jnp.stack(
        [jnp.sum(cotangent * const_wide[i], axis=-1) for i in range(consts)], axis=-1
    )
    grad_rows = grad_total[:pos_count]
    expert_dot = jnp.stack(
        [grad_total[pos_count, i * pos_count : (i + 1) * pos_count] for i in range(2)], axis=-1
    )
    grad_gates = (
        expert_dot
        + one_hot[..., EXPERTS + 1] * copy_dot[:, None]
        + jnp.sum(one_hot[..., EXPERTS + 2 :] * const_dot[:, None, :], axis=-1)
    )
    grad_chosen = gate_probs * (
        grad_gates - jnp.sum(gate_probs * grad_gates, axis=-1, keepdims=True)
    )
    prior_logits_gradient = jnp.sum(one_hot * grad_chosen[..., None], axis=1)
    highest = lax.Precision.HIGHEST
    grad_normed_two = (
        grad_rows
        + copies * cotangent
        + jnp.einsum("wk,ok->wo", prior_logits_gradient, router_wide, precision=highest)
    )
    router_part = jnp.einsum(
        "rx,rb->xb", normed_low.astype(jnp.float32), prior_logits_gradient, precision=highest
    )
    const_part = jnp.einsum("rx,rb->xb", cotangent, const_probs, precision=highest)
    moe_gain_part = jnp.sum(grad_normed_two * scaled_two, axis=0)
    grad_middle = cotangent + rms_back(grad_normed_two * gain_moe, middle, inverse_two)
    grad_projected = grad_middle.astype(jnp.bfloat16)
    small_early = jnp.concatenate(
        [router_part, const_part, jnp.zeros_like(moe_gain_part)[:, None], moe_gain_part[:, None]],
        axis=1,
    )
    small_early = jnp.pad(small_early, ((0, 0), (0, 128 - small_count)))
    output_part = dot_tall(mixed_heads.astype(jnp.bfloat16), grad_projected)
    output_mine, output_other = split_core(output_part.astype(jnp.bfloat16), core_place)
    grad_projected, out_other, output_mine, output_other, small_early = together(
        grad_projected, out_other, output_mine, output_other, small_early
    )
    kept = [query_rot, keys_all, values_all, mixed_heads, totals]
    shared_args = [place, normed_all, gathered, cosine, sine, segment_column, segment_low, kept]
    out_total = add_low(out_parts[3], out_other)
    out_passed, out_other = along_z(out_total, -1), across_x(out_parts[6])
    output_other = across_core(output_other)
    grads_a = attention_backward(*shared_args, grad_projected, 0, 2)
    grad_projected, grads_a, out_passed, out_other, output_other, wide_sum = together(
        grad_projected, grads_a, out_passed, out_other, output_other, wide_sum
    )
    moved_back = [wide_sum[0], along_z(wide_sum[1], -1)]
    out_total = add_all(out_parts[2], out_passed, out_other).astype(jnp.bfloat16)
    output_sum = add_low(output_mine, output_other)
    out_passed, out_other = along_z(out_total, -1), across_x(out_parts[5])
    other_a = across_core(grads_a[1])
    grads_b = attention_backward(*shared_args, grad_projected, 2, 2)
    grad_projected, grads_b, out_passed, out_other, other_a = together(
        grad_projected, grads_b, out_passed, out_other, other_a
    )
    out_total = add_all(out_parts[1], out_passed, out_other).astype(jnp.bfloat16)
    sum_a = add_low(grads_a[0], other_a)
    out_passed, out_other = along_z(out_total, -1), across_x(out_parts[4])
    moved_third = along_z(wide_sum[3], -3)
    other_b = across_core(grads_b[1])
    grads_c = attention_backward(*shared_args, grad_projected, 4, 2)
    grads_c, sum_a, out_passed, out_other, other_b, wide_sum = together(
        grads_c, sum_a, out_passed, out_other, other_b, wide_sum
    )
    moved_back = moved_back + [along_z(wide_sum[2], -2), moved_third]
    down_grad = down_sum.astype(jnp.float32)
    other_c = across_core(grads_c[1])
    sum_b = add_low(grads_b[0], other_b)
    grad_normed_all = grads_a[2] + grads_b[2] + grads_c[2]
    gain_lane = choices + consts
    chosen_lane = jnp.where(jnp.arange(128) == gain_lane, 1.0, 0.0).astype(jnp.bfloat16)
    gain_part = dot_tall(
        (grad_normed_all * scaled_all).astype(jnp.bfloat16),
        jnp.broadcast_to(chosen_lane, (grad_normed_all.shape[0], 128)),
    )
    first_grad = grad_normed_all[:pos_count]
    grad_normed_one = jnp.where(x_place == 0, first_grad, grad_normed_all[pos_count:])
    first_grad = first_grad.astype(jnp.bfloat16)
    small_part = (small_early + gain_part).astype(jnp.bfloat16)
    small_mine, small_other = split_core(small_part, core_place)
    small_sum = add_low(small_mine, across_core(small_other))
    sum_c = add_low(grads_c[0], other_c)
    packed_parts = [part[kind] for kind in range(3) for part in (sum_a, sum_b, sum_c)]
    packed_parts = packed_parts + [output_sum, small_sum]
    packed_grad, shared, moved_back = reduce_packed(
        packed_parts, z_place, y_place, first_grad, moved_back
    )
    const_rows = sum(const_probs[:, i : i + 1] * const_wide[i : i + 1] for i in range(consts))
    layer_out = (
        middle
        + add_all(out_parts[0], out_passed, out_other)
        + copies * normed_two
        + const_rows
    )
    grad_normed_one = grad_normed_one + shared.astype(jnp.float32)
    tokens_grad = grad_middle + rms_back(grad_normed_one * gain_attn, tokens_wide, inverse_one)
    gate_grad, up_grad = place_columns(moved_back, z_place)
    output_grad = packed_grad[:, joint : joint + model_width]
    small_grad = packed_grad[:, joint + model_width :]
    query_grad, key_grad, value_grad = (
        packed_grad[:, i * model_width : (i + 1) * model_width] for i in range(3)
    )
    return (
        layer_out.astype(jnp.bfloat16)[None],
        tokens_grad[None],
        prior_logits_gradient[None],
        query_grad,
        key_grad,
        value_grad,
        output_grad,
        small_grad[:, :choices],
        small_grad[:, choices : choices + consts],
        small_grad[:, choices + consts],
        small_grad[:, choices + consts + 1],
        gate_grad,
        up_grad,
        down_grad,
    )


def solution(mesh):
    in_specs = (
        P("shard", "expert", None),
        P("shard", None),
        P("shard", "expert", None),
        P("shard", "expert", None),
        P("shard", "expert", None),
        P("shard", None),
        P("shard", None),
        P("shard", None),
        P("shard", None),
        P("shard", None),
        P("shard", None),
        P("shard"),
        P("shard"),
        P("expert", "shard", None),
        P("expert", "shard", None),
        P("expert", "shard", None),
    )
    out_specs = (
        P("shard", "expert", None),
        P("shard", "expert", None),
        P("shard", "expert", None),
        P("shard", None),
        P("shard", None),
        P("shard", None),
        P("shard", None),
        P("shard", None),
        P("shard", None),
        P("shard"),
        P("shard"),
        P("expert", "shard", None),
        P("expert", "shard", None),
        P("expert", "shard", None),
    )
    divided = mesh.shape["expert"] == PAIR and mesh.shape["shard"] == RING * PAIR * PAIR
    chosen = body_split if divided else body
    return jax.shard_map(chosen, mesh=mesh, in_specs=in_specs, out_specs=out_specs, check_vma=False)
```

profile of v0, /device:TPU:0, one launch (start us, length us, event | category | flops | bytes accessed | tf_op | source)
XLA Modules:
  0.0 389.7 jit_solution(9237138623786209229)
XLA Ops:
  19.0 12.0 %collective-permute-done.1.refs_1_ = bf16[272,768]{1,0:T(8,128)(2,1)S(1)} collective-permute-done((bf16[272,768]{1,0:T(8,128)(2,1)S(1)}, bf16[272,768]{1,0:T(8,128)(2,1)S(1)}, u32[]{:S(2)}, u32[]{:S(2)}) %collective-permute-start.1) | collective-permute-done | bytes 417824 | tf_op jit(solution)/shard_map/ppermute | solution.py:543
  36.2 11.9 %collective-permute-done.3.refs_2_ = bf16[272,768]{1,0:T(8,128)(2,1)} collective-permute-done((bf16[272,768]{1,0:T(8,128)(2,1)S(1)}, bf16[272,768]{1,0:T(8,128)(2,1)}, u32[]{:S(2)}, u32[]{:S(2)}) %collective-permute-start.3) | collective-permute-done | bytes 417824 | tf_op jit(solution)/shard_map/ppermute | solution.py:543
  51.8 17.7 %collective-permute-done.5.refs_3_ = bf16[272,768]{1,0:T(8,128)(2,1)} collective-permute-done((bf16[272,768]{1,0:T(8,128)(2,1)}, bf16[272,768]{1,0:T(8,128)(2,1)}, u32[]{:S(2)}, u32[]{:S(2)}) %collective-permute-start.5) | collective-permute-done | bytes 417824 | tf_op jit(solution)/shard_map/ppermute | solution.py:543
  74.3 4.2 %collective-permute-done.7.refs_7_ = bf16[272,768]{1,0:T(8,128)(2,1)S(1)} collective-permute-done((bf16[272,768]{1,0:T(8,128)(2,1)}, bf16[272,768]{1,0:T(8,128)(2,1)S(1)}, u32[]{:S(2)}, u32[]{:S(2)}) %collective-permute-start.7) | collective-permute-done | bytes 417824 | tf_op jit(solution)/shard_map/ppermute | solution.py:555
  78.5 11.0 %all-gather.6.cloned.1.call-done.query_weight.key_weight.value_weight.output_weight = bf16[768,3200]{1,0:T(8,128)(2,1)} async-done(((bf16[48,3200]{1,0:T(8,128)(2,1)}), bf16[768,3200]{1,0:T(8,128)(2,1)}) %all-gather.6.cloned.1.call-update) | async-done | bytes 4915216 | tf_op jit(solution)/shard_map/all_gather | solution.py:1272
  98.5 15.2 %attention_forward.1 = (bf16[256,768]{1,0:T(8,128)(2,1)}, bf16[512,768]{1,0:T(8,128)(2,1)}, bf16[512,768]{1,0:T(8,128)(2,1)}, f32[256,768]{1,0:T(8,128)}, f32[6,256,128]{2,1,0:T(8,128)}, /*index=5*/f32[256,768]{1,0:T(8,128)}) custom-call(s32[4]{0:T(128)} %compare_select_fusion.4.place, bf16[512,768]{1,0:T(8,128)(2,1)} %fusion.2.normed_ref, ...), custom_call_target="tpu_custom_call" | custom-call | flops 6000000000 | bytes 45000000 | tf_op jit(solution)/shard_map/attention_forward/pallas_call | solution.py:1127
  118.1 6.9 %collective-permute-start.12 = (bf16[272,768]{1,0:T(8,128)(2,1)S(1)}, bf16[272,768]{1,0:T(8,128)(2,1)}, u32[]{:S(2)}, u32[]{:S(2)}) collective-permute-start(bf16[272,768]{1,0:T(8,128)(2,1)S(1)} %fusion.34.refs_0_), channel_id=1, source_target_pairs={{0,4},{1,5},{2,6},{3,7},{4,8},{5,9},{6,10},{7,11},{8,12},{9,13},{1... | collective-permute-start | bytes 1253384 | tf_op jit(solution)/shard_map/ppermute | solution.py:543
  126.6 7.8 %collective-permute-done.12.refs_1_ = bf16[272,768]{1,0:T(8,128)(2,1)} collective-permute-done((bf16[272,768]{1,0:T(8,128)(2,1)S(1)}, bf16[272,768]{1,0:T(8,128)(2,1)}, u32[]{:S(2)}, u32[]{:S(2)}) %collective-permute-start.12) | collective-permute-done | bytes 417824 | tf_op jit(solution)/shard_map/ppermute | solution.py:543
  138.8 6.3 %pick_slots.1 = (bf16[8,256,256]{2,1,0:T(8,128)(2,1)}, bf16[8,256,768]{2,1,0:T(8,128)(2,1)}) custom-call(s32[4]{0:T(128)} %compare_select_fusion.4.place, bf16[272,768]{1,0:T(8,128)(2,1)} %copy-done.25, bf16[272,768]{1,0:T(8,128)(2,1)} %copy-done.55, bf16[272,768]{1,0:T(8,128)(2,1)} %collective-permute-done.3.refs_2_, ...), custom_call_target="tpu_custom_call" | custom-call | flops 1600000000 | bytes 12000000 | tf_op jit(solution)/shard_map/pick_slots/pallas_call | solution.py:819
  145.1 3.9 %collective-permute-done.14.refs_2_ = bf16[272,768]{1,0:T(8,128)(2,1)} collective-permute-done((bf16[272,768]{1,0:T(8,128)(2,1)}, bf16[272,768]{1,0:T(8,128)(2,1)}, u32[]{:S(2)}, u32[]{:S(2)}) %collective-permute-start.14) | collective-permute-done | bytes 417824 | tf_op jit(solution)/shard_map/ppermute | solution.py:543
  150.8 10.1 %collective-permute-done.16.refs_3_ = bf16[272,768]{1,0:T(8,128)(2,1)S(1)} collective-permute-done((bf16[272,768]{1,0:T(8,128)(2,1)}, bf16[272,768]{1,0:T(8,128)(2,1)S(1)}, u32[]{:S(2)}, u32[]{:S(2)}) %collective-permute-start.16) | collective-permute-done | bytes 417824 | tf_op jit(solution)/shard_map/ppermute | solution.py:543
  162.5 11.3 %prepare_experts.1 = (f32[4,512,512]{2,1,0:T(8,128)}, bf16[4,768,1024]{2,1,0:T(8,128)(2,1)}, bf16[4,512,768]{2,1,0:T(8,128)(2,1)}) custom-call(s32[4]{0:T(128)} %compare_select_fusion.4.place, bf16[8,256,768]{2,1,0:T(8,128)(2,1)} %get-tuple-element.221.slot_ref.refs_1_, bf16[4,2,4,48,512]{4,3,2,1,0:T(8,128)(2,1)} %bitcast.273, ...), custom_call_target="tpu_custom_call" | custom-call | flops 4000000000 | bytes 30000000 | tf_op jit(solution)/shard_map/prepare_experts/pallas_call | solution.py:844
  173.9 22.9 %run_experts.1 = (bf16[8,256,768]{2,1,0:T(8,128)(2,1)}, bf16[4,512,512]{2,1,0:T(8,128)(2,1)}, bf16[4,512,1024]{2,1,0:T(8,128)(2,1)}, bf16[272,768]{1,0:T(8,128)(...) custom-call(s32[4]{0:T(128)} %compare_select_fusion.4.place, ...), custom_call_target="tpu_custom_call" | custom-call | flops 8800000000 | bytes 66000000 | tf_op jit(solution)/shard_map/run_experts/pallas_call | solution.py:881
  197.4 13.0 %weight_grads.1 = (bf16[4,4,2,4,48,512]{5,4,3,2,1,0:T(8,128)(2,1)}, bf16[4,4,128,768]{3,2,1,0:T(8,128)(2,1)}) custom-call(s32[4]{0:T(128)} %compare_select_fusion.4.place, bf16[8,256,768]{2,1,0:T(8,128)(2,1)} %get-tuple-element.233.refs_0_, bf16[8,256,768]{2,1,0:T(8,128)(2,1)} %get-tuple-element.221.slot_ref.refs_1_, ...), custom_call_target="tpu_custom_call" | custom-call | flops 4800000000 | bytes 36000000 | tf_op jit(solution)/shard_map/weight_grads/pallas_call | solution.py:918
  215.0 8.3 %collective-permute-done.23 = bf16[272,768]{1,0:T(8,128)(2,1)S(1)} collective-permute-done((bf16[272,768]{1,0:T(8,128)(2,1)}, bf16[272,768]{1,0:T(8,128)(2,1)S(1)}, u32[]{:S(2)}, u32[]{:S(2)}) %collective-permute-start.23) | collective-permute-done | bytes 417824 | tf_op jit(solution)/shard_map/ppermute | solution.py:555
  232.3 4.3 %collective-permute-done.24 = bf16[272,768]{1,0:T(8,128)(2,1)} collective-permute-done((bf16[272,768]{1,0:T(8,128)(2,1)S(1)}, bf16[272,768]{1,0:T(8,128)(2,1)}, u32[]{:S(2)}, u32[]{:S(2)}) %collective-permute-start.24) | collective-permute-done | bytes 417824 | tf_op jit(solution)/shard_map/ppermute | solution.py:543
  260.0 9.1 %attention_backward.3 = (bf16[3,4,2,48,256]{4,3,2,1,0:T(8,128)(2,1)}, bf16[3,4,2,48,256]{4,3,2,1,0:T(8,128)(2,1)}, f32[512,768]{1,0:T(8,128)}) custom-call(s32[4]{0:T(128)} %compare_select_fusion.4.place, bf16[512,768]{1,0:T(8,128)(2,1)} %fusion.2.normed_ref, ...), custom_call_target="tpu_custom_call" | custom-call | flops 3600000000 | bytes 27000000 | tf_op jit(solution)/shard_map/attention_backward/pallas_call | solution.py:1162
  277.2 9.7 %attention_backward.4 = (bf16[3,4,2,48,256]{4,3,2,1,0:T(8,128)(2,1)}, bf16[3,4,2,48,256]{4,3,2,1,0:T(8,128)(2,1)}, f32[512,768]{1,0:T(8,128)}) custom-call(s32[4]{0:T(128)} %compare_select_fusion.4.place, bf16[512,768]{1,0:T(8,128)(2,1)} %fusion.2.normed_ref, ...), custom_call_target="tpu_custom_call" | custom-call | flops 3600000000 | bytes 27000000 | tf_op jit(solution)/shard_map/attention_backward/pallas_call | solution.py:1162
  295.1 9.2 %attention_backward.5 = (bf16[3,4,2,48,256]{4,3,2,1,0:T(8,128)(2,1)}, bf16[3,4,2,48,256]{4,3,2,1,0:T(8,128)(2,1)}, f32[512,768]{1,0:T(8,128)}) custom-call(s32[4]{0:T(128)} %compare_select_fusion.4.place, bf16[512,768]{1,0:T(8,128)(2,1)} %fusion.2.normed_ref, ...), custom_call_target="tpu_custom_call" | custom-call | flops 3600000000 | bytes 27000000 | tf_op jit(solution)/shard_map/attention_backward/pallas_call | solution.py:1162
  304.3 4.9 %collective-permute-done.35 = bf16[256,768]{1,0:T(8,128)(2,1)S(1)} collective-permute-done((bf16[256,768]{1,0:T(8,128)(2,1)}, bf16[256,768]{1,0:T(8,128)(2,1)S(1)}, u32[]{:S(2)}, u32[]{:S(2)}) %collective-permute-start.35) | collective-permute-done | bytes 393248 | tf_op jit(solution)/shard_map/ppermute | solution.py:543
  328.1 8.0 %collective-permute-done.40 = bf16[48,3200]{1,0:T(8,128)(2,1)S(1)} collective-permute-done((bf16[48,3200]{1,0:T(8,128)(2,1)S(1)}, bf16[48,3200]{1,0:T(8,128)(2,1)S(1)}, u32[]{:S(2)}, u32[]{:S(2)}) %collective-permute-start.40) | collective-permute-done | bytes 307232 | tf_op jit(solution)/shard_map/ppermute | solution.py:547
  342.0 6.3 %collective-permute-done.41 = bf16[48,3200]{1,0:T(8,128)(2,1)S(1)} collective-permute-done((bf16[48,3200]{1,0:T(8,128)(2,1)S(1)}, bf16[48,3200]{1,0:T(8,128)(2,1)S(1)}, u32[]{:S(2)}, u32[]{:S(2)}) %collective-permute-start.41) | collective-permute-done | bytes 307232 | tf_op jit(solution)/shard_map/ppermute | solution.py:543
  353.0 6.0 %collective-permute-done.43 = bf16[48,3200]{1,0:T(8,128)(2,1)S(1)} collective-permute-done((bf16[48,3200]{1,0:T(8,128)(2,1)S(1)}, bf16[48,3200]{1,0:T(8,128)(2,1)S(1)}, u32[]{:S(2)}, u32[]{:S(2)}) %collective-permute-start.43) | collective-permute-done | bytes 307232 | tf_op jit(solution)/shard_map/ppermute | solution.py:543
  371.5 5.9 %collective-permute-done.51 = bf16[48,3200]{1,0:T(8,128)(2,1)S(1)} collective-permute-done((bf16[48,3200]{1,0:T(8,128)(2,1)S(1)}, bf16[48,3200]{1,0:T(8,128)(2,1)S(1)}, u32[]{:S(2)}, u32[]{:S(2)}) %collective-permute-start.51) | collective-permute-done | bytes 307232 | tf_op jit(solution)/shard_map/ppermute | solution.py:555
  (351 shorter events, 148.4 us)
Async XLA Ops:
  7.2 82.3 %all-gather.6.cloned.1.call-start = ((), (), s32[]{:S(2)}) async-start(), calls=%async_computation.2 | async-start | bytes 5222400 | tf_op jit(solution)/shard_map/all_gather | solution.py:1272
  12.5 150.0 %all-gather.8.cloned.1.call-start = ((), (), s32[]{:S(2)}) async-start(), calls=%async_computation.5 | async-start | bytes 1966080 | tf_op jit(solution)/shard_map/all_gather | solution.py:604
  34.6 54.9 %collective-permute-start.8 = (bf16[4,128,768]{2,1,0:T(8,128)(2,1)}, bf16[4,128,768]{2,1,0:T(8,128)(2,1)}, u32[]{:S(2)}, u32[]{:S(2)}) collective-permute-start(bf16[4,128,768]{2,1,0:T(8,128)(2,1)} %refs_0_.1), channel_id=1, source_target_pairs={{0,2},{1,3},{2,0},{3,1},{4,6},{5,7},{6,4},{7,5},{8,10},{9,11},{10,... | collective-permute-start | bytes 2359304 | tf_op jit(solution)/shard_map/ppermute | solution.py:547
  48.1 21.4 %collective-permute-start.5 = (bf16[272,768]{1,0:T(8,128)(2,1)}, bf16[272,768]{1,0:T(8,128)(2,1)}, u32[]{:S(2)}, u32[]{:S(2)}) collective-permute-start(bf16[272,768]{1,0:T(8,128)(2,1)} %collective-permute-done.3.refs_2_), channel_id=1, source_target_pairs={{0,4},{1,5},{2,6},{3,7},{4,8},{5,9},{6,10},{7,11},{8,12},{9,13},{1... | collective-permute-start | bytes 1253384 | tf_op jit(solution)/shard_map/ppermute | solution.py:543
  48.1 21.4 %collective-permute-start.6 = (bf16[272,768]{1,0:T(8,128)(2,1)}, bf16[272,768]{1,0:T(8,128)(2,1)S(1)}, u32[]{:S(2)}, u32[]{:S(2)}) collective-permute-start(bf16[272,768]{1,0:T(8,128)(2,1)} %collective-permute-done.3.refs_2_), channel_id=1, source_target_pairs={{0,16},{16,0},{1,17},{17,1},{2,18},{18,2},{3,19},{19,3},{4,20},{20... | collective-permute-start | bytes 1253384 | tf_op jit(solution)/shard_map/ppermute | solution.py:555
  49.9 39.6 %collective-permute-start.9 = (bf16[2,4,48,512]{3,2,1,0:T(8,128)(2,1)S(1)}, bf16[2,4,48,512]{3,2,1,0:T(8,128)(2,1)S(1)}, u32[]{:S(2)}, u32[]{:S(2)}) collective-permute-start(bf16[2,4,48,512]{3,2,1,0:T(8,128)(2,1)S(1)} %pad_maximum_fusion.3), channel_id=1, source_target_pairs={{0,4},{1,5},{2,6},{3,7},{4,8},{5,9},{6,10},{7,11},{8,12},{9,13},{1... | collective-permute-start | bytes 1179656 | tf_op jit(solution)/shard_map/ppermute | solution.py:543
  51.2 23.1 %collective-permute-start = (bf16[256,768]{1,0:T(8,128)(2,1)S(1)}, bf16[256,768]{1,0:T(8,128)(2,1)S(1)}, u32[]{:S(2)}, u32[]{:S(2)}) collective-permute-start(bf16[256,768]{1,0:T(8,128)(2,1)S(1)} %bitcast.255), channel_id=1, source_target_pairs={{0,16},{16,0},{1,17},{17,1},{2,18},{18,2},{3,19},{19,3},{4,20},{20... | collective-permute-start | bytes 1179656 | tf_op jit(solution)/shard_map/ppermute | solution.py:555
  89.5 73.0 %all-gather.10.cloned.1.call-start = ((), (), s32[]{:S(2)}) async-start(), calls=%async_computation.6 | async-start | bytes 5898240 | tf_op jit(solution)/shard_map/all_gather | solution.py:604
  91.6 22.1 %collective-permute-start.10 = (bf16[2,4,48,512]{3,2,1,0:T(8,128)(2,1)S(1)}, bf16[2,4,48,512]{3,2,1,0:T(8,128)(2,1)S(1)}, u32[]{:S(2)}, u32[]{:S(2)}) collective-permute-start(bf16[2,4,48,512]{3,2,1,0:T(8,128)(2,1)S(1)} %pad_maximum_fusion.4), channel_id=1, source_target_pairs={{0,8},{1,9},{2,10},{3,11},{4,12},{5,13},{6,14},{7,15},{8,0},{9,1},... | collective-permute-start | bytes 1179656 | tf_op jit(solution)/shard_map/ppermute | solution.py:543
  92.2 21.5 %collective-permute-start.11 = (bf16[2,4,48,512]{3,2,1,0:T(8,128)(2,1)S(1)}, bf16[2,4,48,512]{3,2,1,0:T(8,128)(2,1)S(1)}, u32[]{:S(2)}, u32[]{:S(2)}) collective-permute-start(bf16[2,4,48,512]{3,2,1,0:T(8,128)(2,1)S(1)} %pad_maximum_fusion.5), channel_id=1, source_target_pairs={{0,12},{1,13},{2,14},{3,15},{4,0},{5,1},{6,2},{7,3},{8,4},{9,5},{1... | collective-permute-start | bytes 1179656 | tf_op jit(solution)/shard_map/ppermute | solution.py:543
  114.8 154.3 %reduce-scatter.3.cloned.1.call-start = ((), (), s32[]{:S(2)}) async-start(), calls=%async_computation.3 | async-start | bytes 7864320 | tf_op jit(solution)/shard_map/reduce_scatter | solution.py:598
  138.3 24.2 %collective-permute-start.19 = (bf16[4,128,768]{2,1,0:T(8,128)(2,1)S(1)}, bf16[4,128,768]{2,1,0:T(8,128)(2,1)}, u32[]{:S(2)}, u32[]{:S(2)}) collective-permute-start(bf16[4,128,768]{2,1,0:T(8,128)(2,1)S(1)} %copy-done.54), channel_id=1, source_target_pairs={{0,1},{1,0},{2,3},{3,2},{4,5},{5,4},{6,7},{7,6},{8,9},{9,8},{10,11... | collective-permute-start | bytes 2359304 | tf_op jit(solution)/shard_map/ppermute | solution.py:551
  138.3 24.2 %collective-permute-start.20 = (bf16[4,128,768]{2,1,0:T(8,128)(2,1)}, bf16[4,128,768]{2,1,0:T(8,128)(2,1)}, u32[]{:S(2)}, u32[]{:S(2)}) collective-permute-start(bf16[4,128,768]{2,1,0:T(8,128)(2,1)} %collective-permute-done.8.refs_1_), channel_id=1, source_target_pairs={{0,1},{1,0},{2,3},{3,2},{4,5},{5,4},{6,7},{7,6},{8,9},{9,8},{10,11... | collective-permute-start | bytes 2359304 | tf_op jit(solution)/shard_map/ppermute | solution.py:551
  210.5 169.9 %reduce-scatter.5.cloned.1.call-start = ((), (), s32[]{:S(2)}) async-start(), calls=%async_computation.4 | async-start | bytes 3932160 | tf_op jit(solution)/shard_map/reduce_scatter | solution.py:598
  214.2 18.1 %collective-permute-start.25 = (bf16[272,768]{1,0:T(8,128)(2,1)}, bf16[272,768]{1,0:T(8,128)(2,1)S(1)}, u32[]{:S(2)}, u32[]{:S(2)}) collective-permute-start(bf16[272,768]{1,0:T(8,128)(2,1)} %get-tuple-element.242), channel_id=1, source_target_pairs={{0,16},{16,0},{1,17},{17,1},{2,18},{18,2},{3,19},{19,3},{4,20},{20... | collective-permute-start | bytes 1253384 | tf_op jit(solution)/shard_map/ppermute | solution.py:555
  241.8 27.3 %collective-permute-start.30 = (bf16[256,768]{1,0:T(8,128)(2,1)}, bf16[256,768]{1,0:T(8,128)(2,1)}, u32[]{:S(2)}, u32[]{:S(2)}) collective-permute-start(bf16[256,768]{1,0:T(8,128)(2,1)} %get-tuple-element.271), channel_id=1, source_target_pairs={{0,16},{16,0},{1,17},{17,1},{2,18},{18,2},{3,19},{19,3},{4,20},{20... | collective-permute-start | bytes 1179656 | tf_op jit(solution)/shard_map/ppermute | solution.py:555
  251.9 17.3 %collective-permute-start.31 = (bf16[4,2,48,768]{3,2,1,0:T(8,128)(2,1)}, bf16[4,2,48,768]{3,2,1,0:T(8,128)(2,1)S(1)}, u32[]{:S(2)}, u32[]{:S(2)}) collective-permute-start(bf16[4,2,48,768]{3,2,1,0:T(8,128)(2,1)} %fusion.31), channel_id=1, source_target_pairs={{0,1},{1,0},{2,3},{3,2},{4,5},{5,4},{6,7},{7,6},{8,9},{9,8},{10,11... | collective-permute-start | bytes 1769480 | tf_op jit(solution)/shard_map/ppermute | solution.py:551
  257.3 29.6 %collective-permute-start.33 = (bf16[256,768]{1,0:T(8,128)(2,1)}, bf16[256,768]{1,0:T(8,128)(2,1)}, u32[]{:S(2)}, u32[]{:S(2)}) collective-permute-start(bf16[256,768]{1,0:T(8,128)(2,1)} %get-tuple-element.283), channel_id=1, source_target_pairs={{0,16},{16,0},{1,17},{17,1},{2,18},{18,2},{3,19},{19,3},{4,20},{20... | collective-permute-start | bytes 1179656 | tf_op jit(solution)/shard_map/ppermute | solution.py:555
  259.2 45.1 %collective-permute-start.36 = (bf16[256,768]{1,0:T(8,128)(2,1)}, bf16[256,768]{1,0:T(8,128)(2,1)S(1)}, u32[]{:S(2)}, u32[]{:S(2)}) collective-permute-start(bf16[256,768]{1,0:T(8,128)(2,1)} %get-tuple-element.294), channel_id=1, source_target_pairs={{0,16},{16,0},{1,17},{17,1},{2,18},{18,2},{3,19},{19,3},{4,20},{20... | collective-permute-start | bytes 1179656 | tf_op jit(solution)/shard_map/ppermute | solution.py:555
  271.4 16.7 %collective-permute-start.32 = (bf16[256,768]{1,0:T(8,128)(2,1)}, bf16[256,768]{1,0:T(8,128)(2,1)}, u32[]{:S(2)}, u32[]{:S(2)}) collective-permute-start(bf16[256,768]{1,0:T(8,128)(2,1)} %add_convert_fusion.9), channel_id=1, source_target_pairs={{0,12},{1,13},{2,14},{3,15},{4,0},{5,1},{6,2},{7,3},{8,4},{9,5},{1... | collective-permute-start | bytes 1179656 | tf_op jit(solution)/shard_map/ppermute | solution.py:543
  275.7 83.5 %collective-permute-start.46 = (bf16[2,4,48,512]{3,2,1,0:T(8,128)(2,1)}, bf16[2,4,48,512]{3,2,1,0:T(8,128)(2,1)}, u32[]{:S(2)}, u32[]{:S(2)}) collective-permute-start(bf16[2,4,48,512]{3,2,1,0:T(8,128)(2,1)} %get-tuple-element.428), channel_id=1, source_target_pairs={{0,12},{1,13},{2,14},{3,15},{4,0},{5,1},{6,2},{7,3},{8,4},{9,5},{1... | collective-permute-start | bytes 1179656 | tf_op jit(solution)/shard_map/ppermute | solution.py:543
  286.9 72.2 %collective-permute-start.48 = (bf16[2,4,48,512]{3,2,1,0:T(8,128)(2,1)}, bf16[2,4,48,512]{3,2,1,0:T(8,128)(2,1)}, u32[]{:S(2)}, u32[]{:S(2)}) collective-permute-start(bf16[2,4,48,512]{3,2,1,0:T(8,128)(2,1)} %get-tuple-element.427), channel_id=1, source_target_pairs={{0,4},{1,5},{2,6},{3,7},{4,8},{5,9},{6,10},{7,11},{8,12},{9,13},{1... | collective-permute-start | bytes 1179656 | tf_op jit(solution)/shard_map/ppermute | solution.py:543
  290.1 19.2 %collective-permute-start.35 = (bf16[256,768]{1,0:T(8,128)(2,1)}, bf16[256,768]{1,0:T(8,128)(2,1)S(1)}, u32[]{:S(2)}, u32[]{:S(2)}) collective-permute-start(bf16[256,768]{1,0:T(8,128)(2,1)} %add_convert_fusion.8), channel_id=1, source_target_pairs={{0,12},{1,13},{2,14},{3,15},{4,0},{5,1},{6,2},{7,3},{8,4},{9,5},{1... | collective-permute-start | bytes 1179656 | tf_op jit(solution)/shard_map/ppermute | solution.py:543
  321.2 38.0 %collective-permute-start.47 = (bf16[2,4,48,512]{3,2,1,0:T(8,128)(2,1)S(1)}, bf16[2,4,48,512]{3,2,1,0:T(8,128)(2,1)S(1)}, u32[]{:S(2)}, u32[]{:S(2)}) collective-permute-start(bf16[2,4,48,512]{3,2,1,0:T(8,128)(2,1)S(1)} %slice_bitcast_fusion.4), channel_id=1, source_target_pairs={{0,8},{1,9},{2,10},{3,11},{4,12},{5,13},{6,14},{7,15},{8,0},{9,1},... | collective-permute-start | bytes 1179656 | tf_op jit(solution)/shard_map/ppermute | solution.py:543
  (95 other events, 1050.6 us)
Sparse Core Ops, SparseCore 0:
  12.6 76.8 all-gather.5
  91.1 17.9 all-gather.7
  115.0 42.0 all-gather.9
  210.6 58.4 reduce-scatter.2
  276.4 36.0 reduce-scatter.4
where the time goes:
time: 398 us; the launch traced here: 390 us
  waiting for transfers between devices  139 us (35%)
  Pallas kernels  96.6 us (24%)
  starting transfers between devices  70.3 us (18%)
  other arithmetic  38 us (10%)
  local copies, waits for them, and re-layouts  25.9 us (7%)
  between operations  15.3 us (4%)
  matrix products  4.36 us (1%)
    ppermute x21, waiting for transfers between devices, along_z(): return lax.ppermute(values, 'shard', z_pairs(step))  91.5 us
    ppermute x21, starting transfers between devices, along_z(): return lax.ppermute(values, 'shard', z_pairs(step))  41.8 us
    pallas_call x3, Pallas kernels, attention_backward(): pl.pallas_call(attention_backward_kernel, name='attention_backward', cost...  28 us
    ppermute x18, waiting for transfers between devices, across_x(): return lax.ppermute(values, 'expert', [(0, 1), (1, 0)])  24.1 us
    pallas_call x1, Pallas kernels, run_experts(): pl.pallas_call(expert_kernel, name='run_experts', cost_estimate=busy(22),...  22.9 us
    ppermute x18, starting transfers between devices, across_x(): return lax.ppermute(values, 'expert', [(0, 1), (1, 0)])  21.4 us
    pallas_call x1, Pallas kernels, attention_forward(): pl.pallas_call(attention_forward_kernel, name='attention_forward', cost_e...  15.2 us
    pallas_call x1, Pallas kernels, weight_grads(): pl.pallas_call(weight_grad_kernel, name='weight_grads', cost_estimate=bus...  13 us
  transfers between devices with their start and end apart: 57, of which 21 were waited for; matrix products, arithmetic and copies ran while one was open for 14% of the time, Pallas kernels for 19%

commit v1 on v0

--- a/solution.py
+++ b/solution.py
@@ -612,7 +612,7 @@
     return mine, other
 
 
-def reduce_packed(parts, z_place, y_place, first_grad, late):
+def reduce_packed(parts, z_place, y_place, first_grad, late, finish):
     total = None
     for step in reversed(range(RING)):
         owner = lax.rem(z_place - step + RING, RING)
@@ -621,13 +621,16 @@
         other = across_y(jnp.where(y_place == 0, block[1], block[0]))
         mine = jnp.where(y_place == 0, block[0], block[1])
         if total is None:
-            other, first_grad = together(other, first_grad)
+            other, first_grad, passed = together(other, first_grad, late[1])
+            late = (late[0], passed)
             here = add_all(mine, other)
             shared = lax.ppermute(first_grad, "expert", [(1, 0)])
         else:
             passed, other = together(along_z(total, -1), other)
             if step == 1:
                 passed, shared, late = together(passed, shared, late)
+            if step == 0:
+                passed, late = together(passed, finish(late))
             here = add_all(mine, passed, other)
         total = here.astype(jnp.bfloat16)
     return add_all(total, across_x(total)), shared, late
@@ -655,7 +658,7 @@
 def pick_kernel(place, *refs):
     block_count = RING * PAIR
     grads = refs[:block_count]
-    pick_ref, slot_ref = refs[block_count:]
+    pick_ref, slot_ref, stage = refs[block_count:]
     rows = pick_ref.shape[2]
     later = lax.broadcasted_iota(jnp.int32, (rows, rows), 1)
     earlier = lax.broadcasted_iota(jnp.int32, (rows, rows), 0)
@@ -666,7 +669,10 @@
     inside = lax.broadcasted_iota(jnp.int32, (8, rows), 0) < LOCAL
     ranks = lax.broadcasted_iota(jnp.int32, (CAP, rows), 0).astype(jnp.float32)
     for block in range(block_count):
-        meta = grads[block][rows : rows + META, :].astype(jnp.float32)
+        stage[block] = grads[block][...]
+
+    def fill(block, nothing):
+        meta = stage[block, rows : rows + META, :].astype(jnp.float32)
         first = meta[1:2, :rows]
         second = meta[1:2, rows : 2 * rows]
         named = jnp.where(((first == wanted) | (second == wanted)) & inside, 1.0, 0.0)
@@ -677,7 +683,10 @@
             pieces.append(jnp.where(hit, 1.0, 0.0))
         pick = jnp.concatenate(pieces, axis=0).astype(jnp.bfloat16)
         pick_ref[block] = pick
-        slot_ref[block] = dot_rows(pick, grads[block][:rows, :]).astype(jnp.bfloat16)
+        slot_ref[block] = dot_rows(pick, stage[block, :rows, :]).astype(jnp.bfloat16)
+        return nothing
+
+    lax.fori_loop(0, block_count, fill, 0)
 
 
 def prepare_kernel(place, slot_ref, own_ref, moved_ref, *refs):
@@ -711,7 +720,7 @@
     slot_ref, hidden_ref, mixed_ref = rest[:3]
     grad_refs = rest[3 : 3 + block_count]
     out_refs = rest[3 + block_count : 3 + 2 * block_count]
-    out_slots, grad_slots, gate_grads = rest[3 + 2 * block_count :]
+    out_slots, grad_slots, gate_grads, stage, product_ref, chance_ref = rest[3 + 2 * block_count :]
     number = pl.program_id(0)
     rows = pick_ref.shape[2]
     width = slot_ref.shape[2]
@@ -721,9 +730,15 @@
     def _():
         gate_grads[...] = jnp.zeros_like(gate_grads)
         for block in range(block_count):
-            slot_ref[block] = dot_rows(pick_ref[block], tokens[block][:rows, :]).astype(
+            stage[block] = tokens[block][...]
+
+        def gather(block, nothing):
+            slot_ref[block] = dot_rows(pick_ref[block], stage[block, :rows, :]).astype(
                 jnp.bfloat16
             )
+            return nothing
+
+        lax.fori_loop(0, block_count, gather, 0)
 
     span = pl.ds(pl.multiple_of(number * CAP, CAP), CAP)
     mine = slot_ref[:, span, :].reshape(block_count * CAP, width)
@@ -735,21 +750,23 @@
     hidden = silu * up
     back = back_ref[0]
     expert_id = (number + place[0] * LOCAL).astype(jnp.float32)
-    chances = []
-    product = jnp.sum(hidden * back, axis=1, keepdims=True)
-    for block in range(block_count):
-        meta = tokens[block][rows : rows + META, :].astype(jnp.float32)
+    product_ref[...] = jnp.sum(hidden * back, axis=1, keepdims=True)
+
+    def spread_block(block, nothing):
+        meta = stage[block, rows : rows + META, :].astype(jnp.float32)
         first = jnp.where(meta[1:2, :rows] == expert_id, 1.0, 0.0)
         second = jnp.where(meta[1:2, rows : 2 * rows] == expert_id, 1.0, 0.0)
         pick = pick_ref[block, span, :].astype(jnp.float32)
         chance = first * meta[0:1, :rows] + second * meta[0:1, rows : 2 * rows]
-        chances.append(jnp.sum(pick * chance, axis=1, keepdims=True))
-        spread = jnp.sum(
-            pick * product[block * CAP : (block + 1) * CAP], axis=0, keepdims=True
-        )
+        slots = pl.ds(pl.multiple_of(block * CAP, CAP), CAP)
+        chance_ref[slots, :] = jnp.sum(pick * chance, axis=1, keepdims=True)
+        spread = jnp.sum(pick * product_ref[slots, :], axis=0, keepdims=True)
         gate_grads[block, 0:1, :rows] += first * spread
         gate_grads[block, 0:1, rows : 2 * rows] += second * spread
-    chance = jnp.concatenate(chances, axis=0)
+        return nothing
+
+    lax.fori_loop(0, block_count, spread_block, 0, unroll=4)
+    chance = chance_ref[...]
     back = back * chance
     weighted = (hidden * chance).astype(jnp.bfloat16)
     grad_gate = back * up * sigmoid * (1.0 + gate * (1.0 - sigmoid))
@@ -764,15 +781,21 @@
 
     @pl.when(number == LOCAL - 1)
     def _():
+        def scatter(block, nothing):
+            pick = pick_ref[block]
+            grad_slots[block] = dot_tall(pick, grad_slots[block]).astype(jnp.bfloat16)
+            out_slots[block] = dot_tall(pick, out_slots[block]).astype(jnp.bfloat16)
+            return nothing
+
+        lax.fori_loop(0, block_count, scatter, 0)
         for block in range(block_count):
-            pick = pick_ref[block]
-            grad_refs[block][:rows, :] = dot_tall(pick, grad_slots[block]).astype(jnp.bfloat16)
+            grad_refs[block][:rows, :] = grad_slots[block]
             grad_refs[block][rows : rows + META, :] = gate_grads[block].astype(jnp.bfloat16)
-            out_refs[block][...] = dot_tall(pick, out_slots[block]).astype(jnp.bfloat16)
+            out_refs[block][...] = out_slots[block]
 
 
 def weight_grad_kernel(place, *refs):
-    slot_ref, back_ref, hidden_ref, mixed_ref, wide_ref, down_ref, wide_sum = refs
+    slot_ref, back_ref, hidden_ref, mixed_ref, wide_ref, near_ref, core_ref, wide_sum = refs
     number = pl.program_id(0)
     block_count, _, width = slot_ref.shape
     span = pl.ds(pl.multiple_of(number * CAP, CAP), CAP)
@@ -780,7 +803,7 @@
     wide_sum[...] = dot_tall(rows, mixed_ref[0])
     grads = back_ref[:, span, :].reshape(block_count * CAP, width)
     half = wide_sum.shape[1] // 2
-    deep = down_ref.shape[2]
+    deep = near_ref.shape[2]
     depth = wide_ref.shape[4]
     for line in range(PAIR * PAIR):
         for step in range(RING):
@@ -788,8 +811,11 @@
             part = wide_sum[pl.ds(pl.multiple_of(owner * depth, 16), depth), :]
             wide_ref[line, step, 0, 0] = part[:, :half].astype(jnp.bfloat16)
             wide_ref[line, step, 1, 0] = part[:, half:].astype(jnp.bfloat16)
-        columns = hidden_ref[0, :, line * deep : (line + 1) * deep]
-        down_ref[line, 0] = dot_tall(columns, grads).astype(jnp.bfloat16)
+        side, core = line % PAIR, line // PAIR
+        source = (place[2] ^ side) * PAIR + (place[3] ^ core)
+        columns = hidden_ref[0, :, pl.ds(pl.multiple_of(source * deep, deep), deep)]
+        target = core_ref if core else near_ref
+        target[side, 0] = dot_tall(columns, grads).astype(jnp.bfloat16)
 
 
 def busy(microseconds):
@@ -826,6 +852,7 @@
             grid=(1,),
             in_specs=[whole(g.shape) for g in grads],
             out_specs=[whole(shape) for shape in shapes],
+            scratch_shapes=[pltpu.VMEM((blocks, padded, width), jnp.bfloat16)],
         ),
     )(place, *grads)
 
@@ -903,6 +930,9 @@
                 pltpu.VMEM((blocks, local * CAP, width), jnp.bfloat16),
                 pltpu.VMEM((blocks, local * CAP, width), jnp.bfloat16),
                 pltpu.VMEM((blocks, META, width), jnp.float32),
+                pltpu.VMEM((blocks, padded, width), jnp.bfloat16),
+                pltpu.VMEM((slots, 1), jnp.float32),
+                pltpu.VMEM((slots, 1), jnp.float32),
             ],
         ),
     )(place, *tokens, pick, wide, down, back)
@@ -921,7 +951,8 @@
         cost_estimate=busy(12),
         out_shape=[
             jax.ShapeDtypeStruct((lines, RING, 2, local, depth, span), jnp.bfloat16),
-            jax.ShapeDtypeStruct((lines, local, deep, width), jnp.bfloat16),
+            jax.ShapeDtypeStruct((PAIR, local, deep, width), jnp.bfloat16),
+            jax.ShapeDtypeStruct((PAIR, local, deep, width), jnp.bfloat16),
         ],
         grid_spec=pltpu.PrefetchScalarGridSpec(
             num_scalar_prefetch=1,
@@ -934,7 +965,8 @@
             ],
             out_specs=[
                 by_expert((lines, RING, 2, 1, depth, span), 3),
-                by_expert((lines, 1, deep, width), 1),
+                by_expert((PAIR, 1, deep, width), 1),
+                by_expert((PAIR, 1, deep, width), 1),
             ],
             scratch_shapes=[pltpu.VMEM((width, 2 * span), jnp.float32)],
         ),
@@ -1033,6 +1065,7 @@
     mixed_ref,
     total_ref,
     grad_ref,
+    carried_ref,
     weight_mine,
     weight_other,
     result_ref,
@@ -1045,7 +1078,7 @@
     @pl.when(pl.program_id(0) == 0)
     def _():
         bias_ref[...] = mask_bias(place[0], rows, columns, column_ref[own, :], row_ref[...])
-        result_ref[...] = jnp.zeros_like(result_ref)
+        result_ref[...] = carried_ref[...]
 
     normed = normed_ref[...]
     grad = grad_ref[...]
@@ -1153,7 +1186,9 @@
     )(place, normed, weights, weights, weights, weights, cosine, sine, column, row)
 
 
-def attention_backward(place, normed, weights, cosine, sine, column, row, kept, grad, first, count):
+def attention_backward(
+    place, normed, weights, cosine, sine, column, row, kept, grad, carried, first, count
+):
     columns, model = normed.shape
     rows = columns // PAIR
     width = model // (HEADS // 2)
@@ -1162,7 +1197,7 @@
     return pl.pallas_call(
         attention_backward_kernel,
         name="attention_backward",
-        cost_estimate=busy(9),
+        cost_estimate=busy(14),
         out_shape=[
             jax.ShapeDtypeStruct((3, RING, PAIR, depth, width * count), jnp.bfloat16),
             jax.ShapeDtypeStruct((3, RING, PAIR, depth, width * count), jnp.bfloat16),
@@ -1179,6 +1214,7 @@
                 across(rows),
                 pl.BlockSpec((1, rows, width), lambda number, place: (number + first, 0, 0)),
                 whole(grad.shape),
+                whole(carried.shape),
             ],
             out_specs=[
                 pl.BlockSpec((3, RING, PAIR, depth, width), lambda n, place: (0, 0, 0, 0, n)),
@@ -1190,7 +1226,7 @@
                 pltpu.VMEM((model, 3 * width), jnp.float32),
             ],
         ),
-    )(place, normed, weights, weights, weights, weights, cosine, sine, column, row, *kept, grad)
+    )(place, normed, weights, weights, weights, weights, cosine, sine, column, row, *kept, grad, carried)
 
 
 def weight_pieces(gate_weight, up_weight, z_place):
@@ -1295,7 +1331,6 @@
     joint = 3 * model_width
     tail = gathered[:, joint + model_width :].astype(jnp.float32)
     router_low = gathered[:, joint + model_width : joint + model_width + choices]
-    router_wide = tail[:, :choices]
     const_wide = tail[:, choices : choices + consts].T
     gain_attn = tail[:, choices + consts]
     gain_moe = tail[:, choices + consts + 1]
@@ -1340,12 +1375,12 @@
         place, token_blocks, pick, wide_full, down_full, back_hidden
     )
 
-    grad_total, (wide_grads, down_grads), out_parts = reduce_rows(
+    grad_total, (wide_grads, down_near, down_core), out_parts = reduce_rows(
         grad_parts, weight_grads(place, token_slots, back_slots, hidden, mixed), out_parts
     )
     wide_sum = scatter_plane(wide_grads)
-    wide_sum, down_grads = together(wide_sum, down_grads)
-    down_sum = scatter_plane(down_grads)
+    down_core = across_core(down_core)
+    down_far = add_low(down_near[1], down_core[1])
     out_other = across_x(out_parts[7])
 
     cotangent = cotangent_low.astype(jnp.float32)
@@ -1368,16 +1403,14 @@
         grad_gates - jnp.sum(gate_probs * grad_gates, axis=-1, keepdims=True)
     )
     prior_logits_gradient = jnp.sum(one_hot * grad_chosen[..., None], axis=1)
-    highest = lax.Precision.HIGHEST
+    prior_low = prior_logits_gradient.astype(jnp.bfloat16)
     grad_normed_two = (
         grad_rows
         + copies * cotangent
-        + jnp.einsum("wk,ok->wo", prior_logits_gradient, router_wide, precision=highest)
-    )
-    router_part = jnp.einsum(
-        "rx,rb->xb", normed_low.astype(jnp.float32), prior_logits_gradient, precision=highest
-    )
-    const_part = jnp.einsum("rx,rb->xb", cotangent, const_probs, precision=highest)
+        + dot_wide(prior_low, router_low)
+    )
+    router_part = dot_tall(normed_low, prior_low)
+    const_part = dot_tall(cotangent_low, const_probs.astype(jnp.bfloat16))
     moe_gain_part = jnp.sum(grad_normed_two * scaled_two, axis=0)
     grad_middle = cotangent + rms_back(grad_normed_two * gain_moe, middle, inverse_two)
     grad_projected = grad_middle.astype(jnp.bfloat16)
@@ -1396,33 +1429,28 @@
     out_total = add_low(out_parts[3], out_other)
     out_passed, out_other = along_z(out_total, -1), across_x(out_parts[6])
     output_other = across_core(output_other)
-    grads_a = attention_backward(*shared_args, grad_projected, 0, 2)
-    grad_projected, grads_a, out_passed, out_other, output_other, wide_sum = together(
-        grad_projected, grads_a, out_passed, out_other, output_other, wide_sum
-    )
-    moved_back = [wide_sum[0], along_z(wide_sum[1], -1)]
+    nothing = jnp.zeros(normed_all.shape, jnp.float32)
+    grads_a = attention_backward(*shared_args, grad_projected, nothing, 0, 3)
+    grad_projected, grads_a, out_passed, out_other, output_other, wide_sum, down_far = together(
+        grad_projected, grads_a, out_passed, out_other, output_other, wide_sum, down_far
+    )
+    down_far = across_y(down_far)
+    moved_first = along_z(wide_sum[1], -1)
     out_total = add_all(out_parts[2], out_passed, out_other).astype(jnp.bfloat16)
     output_sum = add_low(output_mine, output_other)
     out_passed, out_other = along_z(out_total, -1), across_x(out_parts[5])
     other_a = across_core(grads_a[1])
-    grads_b = attention_backward(*shared_args, grad_projected, 2, 2)
-    grad_projected, grads_b, out_passed, out_other, other_a = together(
-        grad_projected, grads_b, out_passed, out_other, other_a
-    )
+    grads_b = attention_backward(*shared_args, grad_projected, grads_a[2], 3, 3)
+    grads_b, out_passed, out_other, other_a, wide_sum, down_far, moved_first = together(
+        grads_b, out_passed, out_other, other_a, wide_sum, down_far, moved_first
+    )
+    moved_third = along_z(wide_sum[3], -3)
     out_total = add_all(out_parts[1], out_passed, out_other).astype(jnp.bfloat16)
+    out_passed, out_other = along_z(out_total, -1), across_x(out_parts[4])
+    moved_back = [wide_sum[0], moved_first, along_z(wide_sum[2], -2), moved_third]
+    other_b = across_core(grads_b[1])
     sum_a = add_low(grads_a[0], other_a)
-    out_passed, out_other = along_z(out_total, -1), across_x(out_parts[4])
-    moved_third = along_z(wide_sum[3], -3)
-    other_b = across_core(grads_b[1])
-    grads_c = attention_backward(*shared_args, grad_projected, 4, 2)
-    grads_c, sum_a, out_passed, out_other, other_b, wide_sum = together(
-        grads_c, sum_a, out_passed, out_other, other_b, wide_sum
-    )
-    moved_back = moved_back + [along_z(wide_sum[2], -2), moved_third]
-    down_grad = down_sum.astype(jnp.float32)
-    other_c = across_core(grads_c[1])
-    sum_b = add_low(grads_b[0], other_b)
-    grad_normed_all = grads_a[2] + grads_b[2] + grads_c[2]
+    grad_normed_all = grads_b[2]
     gain_lane = choices + consts
     chosen_lane = jnp.where(jnp.arange(128) == gain_lane, 1.0, 0.0).astype(jnp.bfloat16)
     gain_part = dot_tall(
@@ -1435,22 +1463,35 @@
     small_part = (small_early + gain_part).astype(jnp.bfloat16)
     small_mine, small_other = split_core(small_part, core_place)
     small_sum = add_low(small_mine, across_core(small_other))
-    sum_c = add_low(grads_c[0], other_c)
-    packed_parts = [part[kind] for kind in range(3) for part in (sum_a, sum_b, sum_c)]
+    sum_b = add_low(grads_b[0], other_b)
+    packed_parts = [part[kind] for kind in range(3) for part in (sum_a, sum_b)]
     packed_parts = packed_parts + [output_sum, small_sum]
-    packed_grad, shared, moved_back = reduce_packed(
-        packed_parts, z_place, y_place, first_grad, moved_back
+
+    def finish(late):
+        moved_back = late[0]
+        return (
+            *place_columns(moved_back, z_place),
+            add_all(down_near[0], down_core[0], down_far),
+            add_all(out_parts[0], *late[1]),
+        )
+
+    packed_grad, shared, (gate_grad, up_grad, down_grad, out_total) = reduce_packed(
+        packed_parts,
+        z_place,
+        y_place,
+        first_grad,
+        (moved_back, (out_passed, out_other)),
+        finish,
     )
     const_rows = sum(const_probs[:, i : i + 1] * const_wide[i : i + 1] for i in range(consts))
     layer_out = (
         middle
-        + add_all(out_parts[0], out_passed, out_other)
+        + out_total
         + copies * normed_two
         + const_rows
     )
     grad_normed_one = grad_normed_one + shared.astype(jnp.float32)
     tokens_grad = grad_middle + rms_back(grad_normed_one * gain_attn, tokens_wide, inverse_one)
-    gate_grad, up_grad = place_columns(moved_back, z_place)
     output_grad = packed_grad[:, joint : joint + model_width]
     small_grad = packed_grad[:, joint + model_width :]
     query_grad, key_grad, value_grad = (

time: 398 us -> 384 us (0.965); the launches traced: 390 us -> 383 us
  waiting for transfers between devices: 139 us -> 131 us
    pallas_call x1, Pallas kernels: 22.9 us -> 27.9 us  [run_experts(): pl.pallas_call(expert_kernel, name='run_experts', cost_estimate=busy(22),...]
    ppermute x18, waiting for transfers between devices: 24.1 us -> 19.7 us  [across_x(): return lax.ppermute(values, 'expert', [(0, 1), (1, 0)])]
    pallas_call x3 -> x2, Pallas kernels: 28 us -> 24.8 us  [attention_backward(): pl.pallas_call(attention_backward_kernel, name='attention_backward', cost...]
    unnamed x140 -> x133, local copies, waits for them, and re-layouts: 12.2 us -> 10.3 us
    ppermute x5 -> x6, waiting for transfers between devices: 10.4 us -> 12.1 us  [across_y(): lax.ppermute(values, 'shard', [(s, s ^ PAIR) for s in range(RING * PAIR *...]
where the time goes in v1:
time: 384 us; the launch traced here: 383 us
  waiting for transfers between devices  131 us (34%)
  Pallas kernels  100 us (26%)
  starting transfers between devices  72.5 us (19%)
  other arithmetic  36.3 us (9%)
  local copies, waits for them, and re-layouts  24.7 us (6%)
  between operations  14.8 us (4%)
  matrix products  3.84 us (1%)
    ppermute x21, waiting for transfers between devices, along_z(): return lax.ppermute(values, 'shard', z_pairs(step))  87.9 us
    ppermute x21, starting transfers between devices, along_z(): return lax.ppermute(values, 'shard', z_pairs(step))  38.7 us
    pallas_call x1, Pallas kernels, run_experts(): pl.pallas_call(expert_kernel, name='run_experts', cost_estimate=busy(22),...  27.9 us
    pallas_call x2, Pallas kernels, attention_backward(): pl.pallas_call(attention_backward_kernel, name='attention_backward', cost...  24.8 us
    ppermute x18, starting transfers between devices, across_x(): return lax.ppermute(values, 'expert', [(0, 1), (1, 0)])  24.6 us
    ppermute x18, waiting for transfers between devices, across_x(): return lax.ppermute(values, 'expert', [(0, 1), (1, 0)])  19.7 us
    pallas_call x1, Pallas kernels, attention_forward(): pl.pallas_call(attention_forward_kernel, name='attention_forward', cost_e...  15.2 us
    pallas_call x1, Pallas kernels, weight_grads(): pl.pallas_call(weight_grad_kernel, name='weight_grads', cost_estimate=bus...  13.1 us
  transfers between devices with their start and end apart: 57, of which 21 were waited for; matrix products, arithmetic and copies ran while one was open for 14% of the time, Pallas kernels for 19%

profile of v1, /device:TPU:0, one launch (start us, length us, event | category | flops | bytes accessed | tf_op | source)
XLA Modules:
  0.0 383.1 jit_solution(384176191938231945)
XLA Ops:
  14.4 3.1 collective-permute-start.1
  19.0 12.0 %collective-permute-done.1.refs_1_ = bf16[272,768]{1,0:T(8,128)(2,1)S(1)} collective-permute-done((bf16[272,768]{1,0:T(8,128)(2,1)S(1)}, bf16[272,768]{1,0:T(8,128)(2,1)S(1)}, u32[]{:S(2)}, u32[]{:S(2)}) %collective-permute-start.1) | collective-permute-done | bytes 417824 | tf_op jit(solution)/shard_map/ppermute | solution.py:543
  36.1 11.9 %collective-permute-done.3.refs_2_ = bf16[272,768]{1,0:T(8,128)(2,1)} collective-permute-done((bf16[272,768]{1,0:T(8,128)(2,1)S(1)}, bf16[272,768]{1,0:T(8,128)(2,1)}, u32[]{:S(2)}, u32[]{:S(2)}) %collective-permute-start.3) | collective-permute-done | bytes 417824 | tf_op jit(solution)/shard_map/ppermute | solution.py:543
  51.8 17.7 %collective-permute-done.5.refs_3_ = bf16[272,768]{1,0:T(8,128)(2,1)} collective-permute-done((bf16[272,768]{1,0:T(8,128)(2,1)}, bf16[272,768]{1,0:T(8,128)(2,1)}, u32[]{:S(2)}, u32[]{:S(2)}) %collective-permute-start.5) | collective-permute-done | bytes 417824 | tf_op jit(solution)/shard_map/ppermute | solution.py:543
  74.3 4.3 %collective-permute-done.7.refs_7_ = bf16[272,768]{1,0:T(8,128)(2,1)} collective-permute-done((bf16[272,768]{1,0:T(8,128)(2,1)}, bf16[272,768]{1,0:T(8,128)(2,1)}, u32[]{:S(2)}, u32[]{:S(2)}) %collective-permute-start.7) | collective-permute-done | bytes 417824 | tf_op jit(solution)/shard_map/ppermute | solution.py:555
  78.6 10.9 %all-gather.6.cloned.1.call-done.query_weight.key_weight.value_weight.output_weight = bf16[768,3200]{1,0:T(8,128)(2,1)} async-done(((bf16[48,3200]{1,0:T(8,128)(2,1)}), bf16[768,3200]{1,0:T(8,128)(2,1)}) %all-gather.6.cloned.1.call-update) | async-done | bytes 4915216 | tf_op jit(solution)/shard_map/all_gather | solution.py:1308
  97.4 15.2 %attention_forward.1 = (bf16[256,768]{1,0:T(8,128)(2,1)}, bf16[512,768]{1,0:T(8,128)(2,1)}, bf16[512,768]{1,0:T(8,128)(2,1)}, f32[256,768]{1,0:T(8,128)}, f32[6,256,128]{2,1,0:T(8,128)}, /*index=5*/f32[256,768]{1,0:T(8,128)}) custom-call(s32[4]{0:T(128)} %compare_select_fusion.4.place, bf16[512,768]{1,0:T(8,128)(2,1)} %fusion.2.normed_ref, ...), custom_call_target="tpu_custom_call" | custom-call | flops 6000000000 | bytes 45000000 | tf_op jit(solution)/shard_map/attention_forward/pallas_call | solution.py:1160
  117.0 8.0 %collective-permute-start.12 = (bf16[272,768]{1,0:T(8,128)(2,1)S(1)}, bf16[272,768]{1,0:T(8,128)(2,1)S(1)}, u32[]{:S(2)}, u32[]{:S(2)}) collective-permute-start(bf16[272,768]{1,0:T(8,128)(2,1)S(1)} %fusion.33.refs_0_), channel_id=1, source_target_pairs={{0,4},{1,5},{2,6},{3,7},{4,8},{5,9},{6,10},{7,11},{8,12},{9,13},{1... | collective-permute-start | bytes 1253384 | tf_op jit(solution)/shard_map/ppermute | solution.py:543
  126.5 7.7 %collective-permute-done.12.refs_1_ = bf16[272,768]{1,0:T(8,128)(2,1)S(1)} collective-permute-done((bf16[272,768]{1,0:T(8,128)(2,1)S(1)}, bf16[272,768]{1,0:T(8,128)(2,1)S(1)}, u32[]{:S(2)}, u32[]{:S(2)}) %collective-permute-start.12) | collective-permute-done | bytes 417824 | tf_op jit(solution)/shard_map/ppermute | solution.py:543
  138.7 7.9 %pick_slots.1 = (bf16[8,256,256]{2,1,0:T(8,128)(2,1)}, bf16[8,256,768]{2,1,0:T(8,128)(2,1)}) custom-call(s32[4]{0:T(128)} %compare_select_fusion.4.place, bf16[272,768]{1,0:T(8,128)(2,1)} %copy-done.26, bf16[272,768]{1,0:T(8,128)(2,1)} %copy-done.50, bf16[272,768]{1,0:T(8,128)(2,1)} %collective-permute-done.3.refs_2_, ...), custom_call_target="tpu_custom_call" | custom-call | flops 1600000000 | bytes 12000000 | tf_op jit(solution)/shard_map/pick_slots/pallas_call | solution.py:845
  150.3 10.2 %collective-permute-done.16.refs_3_ = bf16[272,768]{1,0:T(8,128)(2,1)S(1)} collective-permute-done((bf16[272,768]{1,0:T(8,128)(2,1)}, bf16[272,768]{1,0:T(8,128)(2,1)S(1)}, u32[]{:S(2)}, u32[]{:S(2)}) %collective-permute-start.16) | collective-permute-done | bytes 417824 | tf_op jit(solution)/shard_map/ppermute | solution.py:543
  162.1 11.3 %prepare_experts.1 = (f32[4,512,512]{2,1,0:T(8,128)}, bf16[4,768,1024]{2,1,0:T(8,128)(2,1)}, bf16[4,512,768]{2,1,0:T(8,128)(2,1)}) custom-call(s32[4]{0:T(128)} %compare_select_fusion.4.place, bf16[8,256,768]{2,1,0:T(8,128)(2,1)} %get-tuple-element.222.slot_ref.refs_1_, bf16[4,2,4,48,512]{4,3,2,1,0:T(8,128)(2,1)} %bitcast.247, ...), custom_call_target="tpu_custom_call" | custom-call | flops 4000000000 | bytes 30000000 | tf_op jit(solution)/shard_map/prepare_experts/pallas_call | solution.py:871
  173.5 27.9 %run_experts.1 = (bf16[8,256,768]{2,1,0:T(8,128)(2,1)}, bf16[4,512,512]{2,1,0:T(8,128)(2,1)}, bf16[4,512,1024]{2,1,0:T(8,128)(2,1)}, bf16[272,768]{1,0:T(8,128)(...) custom-call(s32[4]{0:T(128)} %compare_select_fusion.4.place, ...), custom_call_target="tpu_custom_call" | custom-call | flops 8800000000 | bytes 66000000 | tf_op jit(solution)/shard_map/run_experts/pallas_call | solution.py:908
  202.0 13.1 %weight_grads.1 = (bf16[4,4,2,4,48,512]{5,4,3,2,1,0:T(8,128)(2,1)}, bf16[2,4,128,768]{3,2,1,0:T(8,128)(2,1)}, bf16[2,4,128,768]{3,2,1,0:T(8,128)(2,1)}) custom-call(s32[4]{0:T(128)} %compare_select_fusion.4.place, bf16[8,256,768]{2,1,0:T(8,128)(2,1)} %get-tuple-element.236.refs_0_, bf16[8,256,768]{2,1,0:T(8,128)(2,1)} %get-tuple-element.222.slot_ref.refs_1_, ...), custom_call_target="tpu_custom_call" | custom-call | flops 4800000000 | bytes 36000000 | tf_op jit(solution)/shard_map/weight_grads/pallas_call | solution.py:948
  221.6 6.4 %collective-permute-done.23 = bf16[272,768]{1,0:T(8,128)(2,1)S(1)} collective-permute-done((bf16[272,768]{1,0:T(8,128)(2,1)}, bf16[272,768]{1,0:T(8,128)(2,1)S(1)}, u32[]{:S(2)}, u32[]{:S(2)}) %collective-permute-start.23) | collective-permute-done | bytes 417824 | tf_op jit(solution)/shard_map/ppermute | solution.py:555
  228.2 3.8 collective-permute-start.24
  237.9 4.3 %collective-permute-start.26 = (bf16[272,768]{1,0:T(8,128)(2,1)S(1)}, bf16[272,768]{1,0:T(8,128)(2,1)S(1)}, u32[]{:S(2)}, u32[]{:S(2)}) collective-permute-start(bf16[272,768]{1,0:T(8,128)(2,1)S(1)} %add_convert_fusion.4), channel_id=1, source_target_pairs={{0,12},{1,13},{2,14},{3,15},{4,0},{5,1},{6,2},{7,3},{8,4},{9,5},{1... | collective-permute-start | bytes 1253384 | tf_op jit(solution)/shard_map/ppermute | solution.py:543
  259.6 12.4 %attention_backward.2 = (bf16[3,4,2,48,384]{4,3,2,1,0:T(8,128)(2,1)}, bf16[3,4,2,48,384]{4,3,2,1,0:T(8,128)(2,1)}, f32[512,768]{1,0:T(8,128)}) custom-call(s32[4]{0:T(128)} %compare_select_fusion.4.place, bf16[512,768]{1,0:T(8,128)(2,1)} %fusion.2.normed_ref, ...), custom_call_target="tpu_custom_call" | custom-call | flops 5600000000 | bytes 42000000 | tf_op jit(solution)/shard_map/attention_backward/pallas_call | solution.py:1197
  282.5 12.3 %attention_backward.3 = (bf16[3,4,2,48,384]{4,3,2,1,0:T(8,128)(2,1)}, bf16[3,4,2,48,384]{4,3,2,1,0:T(8,128)(2,1)}, f32[512,768]{1,0:T(8,128)}) custom-call(s32[4]{0:T(128)} %compare_select_fusion.4.place, bf16[512,768]{1,0:T(8,128)(2,1)} %fusion.2.normed_ref, ...), custom_call_target="tpu_custom_call" | custom-call | flops 5600000000 | bytes 42000000 | tf_op jit(solution)/shard_map/attention_backward/pallas_call | solution.py:1197
  317.7 8.0 %collective-permute-done.40 = bf16[48,3200]{1,0:T(8,128)(2,1)S(1)} collective-permute-done((bf16[48,3200]{1,0:T(8,128)(2,1)S(1)}, bf16[48,3200]{1,0:T(8,128)(2,1)S(1)}, u32[]{:S(2)}, u32[]{:S(2)}) %collective-permute-start.40) | collective-permute-done | bytes 307232 | tf_op jit(solution)/shard_map/ppermute | solution.py:547
  333.5 10.5 %collective-permute-done.43 = bf16[48,3200]{1,0:T(8,128)(2,1)S(1)} collective-permute-done((bf16[48,3200]{1,0:T(8,128)(2,1)S(1)}, bf16[48,3200]{1,0:T(8,128)(2,1)S(1)}, u32[]{:S(2)}, u32[]{:S(2)}) %collective-permute-start.43) | collective-permute-done | bytes 307232 | tf_op jit(solution)/shard_map/ppermute | solution.py:543
  345.2 8.2 %collective-permute-done.45 = bf16[48,3200]{1,0:T(8,128)(2,1)S(1)} collective-permute-done((bf16[48,3200]{1,0:T(8,128)(2,1)S(1)}, bf16[48,3200]{1,0:T(8,128)(2,1)S(1)}, u32[]{:S(2)}, u32[]{:S(2)}) %collective-permute-start.45) | collective-permute-done | bytes 307232 | tf_op jit(solution)/shard_map/ppermute | solution.py:543
  361.1 4.5 %collective-permute-done.50 = bf16[48,3200]{1,0:T(8,128)(2,1)S(1)} collective-permute-done((bf16[48,3200]{1,0:T(8,128)(2,1)S(1)}, bf16[48,3200]{1,0:T(8,128)(2,1)S(1)}, u32[]{:S(2)}, u32[]{:S(2)}) %collective-permute-start.50) | collective-permute-done | bytes 307232 | tf_op jit(solution)/shard_map/ppermute | solution.py:543
  370.3 3.3 collective-permute-done.52
  (342 shorter events, 133.3 us)
Async XLA Ops:
  7.2 82.3 %all-gather.6.cloned.1.call-start = ((), (), s32[]{:S(2)}) async-start(), calls=%async_computation.1 | async-start | bytes 5222400 | tf_op jit(solution)/shard_map/all_gather | solution.py:1308
  12.5 149.6 %all-gather.8.cloned.1.call-start = ((), (), s32[]{:S(2)}) async-start(), calls=%async_computation.3 | async-start | bytes 1966080 | tf_op jit(solution)/shard_map/all_gather | solution.py:604
  34.6 54.9 %collective-permute-start.8 = (bf16[4,128,768]{2,1,0:T(8,128)(2,1)}, bf16[4,128,768]{2,1,0:T(8,128)(2,1)}, u32[]{:S(2)}, u32[]{:S(2)}) collective-permute-start(bf16[4,128,768]{2,1,0:T(8,128)(2,1)} %refs_0_.1), channel_id=1, source_target_pairs={{0,2},{1,3},{2,0},{3,1},{4,6},{5,7},{6,4},{7,5},{8,10},{9,11},{10,... | collective-permute-start | bytes 2359304 | tf_op jit(solution)/shard_map/ppermute | solution.py:547
  48.1 21.4 %collective-permute-start.5 = (bf16[272,768]{1,0:T(8,128)(2,1)}, bf16[272,768]{1,0:T(8,128)(2,1)}, u32[]{:S(2)}, u32[]{:S(2)}) collective-permute-start(bf16[272,768]{1,0:T(8,128)(2,1)} %collective-permute-done.3.refs_2_), channel_id=1, source_target_pairs={{0,4},{1,5},{2,6},{3,7},{4,8},{5,9},{6,10},{7,11},{8,12},{9,13},{1... | collective-permute-start | bytes 1253384 | tf_op jit(solution)/shard_map/ppermute | solution.py:543
  48.1 21.4 %collective-permute-start.6 = (bf16[272,768]{1,0:T(8,128)(2,1)}, bf16[272,768]{1,0:T(8,128)(2,1)S(1)}, u32[]{:S(2)}, u32[]{:S(2)}) collective-permute-start(bf16[272,768]{1,0:T(8,128)(2,1)} %collective-permute-done.3.refs_2_), channel_id=1, source_target_pairs={{0,16},{16,0},{1,17},{17,1},{2,18},{18,2},{3,19},{19,3},{4,20},{20... | collective-permute-start | bytes 1253384 | tf_op jit(solution)/shard_map/ppermute | solution.py:555
  49.9 39.6 %collective-permute-start.9 = (bf16[2,4,48,512]{3,2,1,0:T(8,128)(2,1)S(1)}, bf16[2,4,48,512]{3,2,1,0:T(8,128)(2,1)S(1)}, u32[]{:S(2)}, u32[]{:S(2)}) collective-permute-start(bf16[2,4,48,512]{3,2,1,0:T(8,128)(2,1)S(1)} %pad_maximum_fusion.3), channel_id=1, source_target_pairs={{0,4},{1,5},{2,6},{3,7},{4,8},{5,9},{6,10},{7,11},{8,12},{9,13},{1... | collective-permute-start | bytes 1179656 | tf_op jit(solution)/shard_map/ppermute | solution.py:543
  51.2 23.1 %collective-permute-start = (bf16[256,768]{1,0:T(8,128)(2,1)S(1)}, bf16[256,768]{1,0:T(8,128)(2,1)S(1)}, u32[]{:S(2)}, u32[]{:S(2)}) collective-permute-start(bf16[256,768]{1,0:T(8,128)(2,1)S(1)} %bitcast.229), channel_id=1, source_target_pairs={{0,16},{16,0},{1,17},{17,1},{2,18},{18,2},{3,19},{19,3},{4,20},{20... | collective-permute-start | bytes 1179656 | tf_op jit(solution)/shard_map/ppermute | solution.py:555
  89.5 72.6 %all-gather.10.cloned.1.call-start = ((), (), s32[]{:S(2)}) async-start(), calls=%async_computation.4 | async-start | bytes 5898240 | tf_op jit(solution)/shard_map/all_gather | solution.py:604
  91.6 21.0 %collective-permute-start.10 = (bf16[2,4,48,512]{3,2,1,0:T(8,128)(2,1)S(1)}, bf16[2,4,48,512]{3,2,1,0:T(8,128)(2,1)S(1)}, u32[]{:S(2)}, u32[]{:S(2)}) collective-permute-start(bf16[2,4,48,512]{3,2,1,0:T(8,128)(2,1)S(1)} %pad_maximum_fusion.4), channel_id=1, source_target_pairs={{0,8},{1,9},{2,10},{3,11},{4,12},{5,13},{6,14},{7,15},{8,0},{9,1},... | collective-permute-start | bytes 1179656 | tf_op jit(solution)/shard_map/ppermute | solution.py:543
  92.2 20.4 %collective-permute-start.11 = (bf16[2,4,48,512]{3,2,1,0:T(8,128)(2,1)S(1)}, bf16[2,4,48,512]{3,2,1,0:T(8,128)(2,1)S(1)}, u32[]{:S(2)}, u32[]{:S(2)}) collective-permute-start(bf16[2,4,48,512]{3,2,1,0:T(8,128)(2,1)S(1)} %pad_maximum_fusion.5), channel_id=1, source_target_pairs={{0,12},{1,13},{2,14},{3,15},{4,0},{5,1},{6,2},{7,3},{8,4},{9,5},{1... | collective-permute-start | bytes 1179656 | tf_op jit(solution)/shard_map/ppermute | solution.py:543
  113.8 161.2 %reduce-scatter.2.cloned.1.call-start = ((), (), s32[]{:S(2)}) async-start(), calls=%async_computation.2 | async-start | bytes 7864320 | tf_op jit(solution)/shard_map/reduce_scatter | solution.py:598
  138.2 23.9 %collective-permute-start.19 = (bf16[4,128,768]{2,1,0:T(8,128)(2,1)S(1)}, bf16[4,128,768]{2,1,0:T(8,128)(2,1)}, u32[]{:S(2)}, u32[]{:S(2)}) collective-permute-start(bf16[4,128,768]{2,1,0:T(8,128)(2,1)S(1)} %copy-done.49), channel_id=1, source_target_pairs={{0,1},{1,0},{2,3},{3,2},{4,5},{5,4},{6,7},{7,6},{8,9},{9,8},{10,11... | collective-permute-start | bytes 2359304 | tf_op jit(solution)/shard_map/ppermute | solution.py:551
  138.2 23.9 %collective-permute-start.20 = (bf16[4,128,768]{2,1,0:T(8,128)(2,1)}, bf16[4,128,768]{2,1,0:T(8,128)(2,1)}, u32[]{:S(2)}, u32[]{:S(2)}) collective-permute-start(bf16[4,128,768]{2,1,0:T(8,128)(2,1)} %collective-permute-done.8.refs_1_), channel_id=1, source_target_pairs={{0,1},{1,0},{2,3},{3,2},{4,5},{5,4},{6,7},{7,6},{8,9},{9,8},{10,11... | collective-permute-start | bytes 2359304 | tf_op jit(solution)/shard_map/ppermute | solution.py:551
  242.9 29.8 %collective-permute-start.32 = (bf16[2,4,128,768]{3,2,1,0:T(8,128)(2,1)}, bf16[2,4,128,768]{3,2,1,0:T(8,128)(2,1)}, u32[]{:S(2)}, u32[]{:S(2)}) collective-permute-start(bf16[2,4,128,768]{3,2,1,0:T(8,128)(2,1)} %get-tuple-element.276), channel_id=1, source_target_pairs={{0,1},{1,0},{2,3},{3,2},{4,5},{5,4},{6,7},{7,6},{8,9},{9,8},{10,11... | collective-permute-start | bytes 4718600 | tf_op jit(solution)/shard_map/ppermute | solution.py:551
  245.1 29.8 %collective-permute-start.30 = (bf16[256,768]{1,0:T(8,128)(2,1)}, bf16[256,768]{1,0:T(8,128)(2,1)}, u32[]{:S(2)}, u32[]{:S(2)}) collective-permute-start(bf16[256,768]{1,0:T(8,128)(2,1)} %get-tuple-element.272), channel_id=1, source_target_pairs={{0,16},{16,0},{1,17},{17,1},{2,18},{18,2},{3,19},{19,3},{4,20},{20... | collective-permute-start | bytes 1179656 | tf_op jit(solution)/shard_map/ppermute | solution.py:555
  245.2 51.2 %collective-permute-start.34 = (bf16[256,768]{1,0:T(8,128)(2,1)}, bf16[256,768]{1,0:T(8,128)(2,1)}, u32[]{:S(2)}, u32[]{:S(2)}) collective-permute-start(bf16[256,768]{1,0:T(8,128)(2,1)} %get-tuple-element.286), channel_id=1, source_target_pairs={{0,16},{16,0},{1,17},{17,1},{2,18},{18,2},{3,19},{19,3},{4,20},{20... | collective-permute-start | bytes 1179656 | tf_op jit(solution)/shard_map/ppermute | solution.py:555
  256.0 19.0 %collective-permute-start.29 = (bf16[256,768]{1,0:T(8,128)(2,1)}, bf16[256,768]{1,0:T(8,128)(2,1)}, u32[]{:S(2)}, u32[]{:S(2)}) collective-permute-start(bf16[256,768]{1,0:T(8,128)(2,1)} %add_convert_fusion.10), channel_id=1, source_target_pairs={{0,12},{1,13},{2,14},{3,15},{4,0},{5,1},{6,2},{7,3},{8,4},{9,5},{1... | collective-permute-start | bytes 1179656 | tf_op jit(solution)/shard_map/ppermute | solution.py:543
  277.3 20.6 %collective-permute-start.33 = (bf16[256,768]{1,0:T(8,128)(2,1)}, bf16[256,768]{1,0:T(8,128)(2,1)}, u32[]{:S(2)}, u32[]{:S(2)}) collective-permute-start(bf16[256,768]{1,0:T(8,128)(2,1)} %add_convert_fusion.9), channel_id=1, source_target_pairs={{0,12},{1,13},{2,14},{3,15},{4,0},{5,1},{6,2},{7,3},{8,4},{9,5},{1... | collective-permute-start | bytes 1179656 | tf_op jit(solution)/shard_map/ppermute | solution.py:543
  279.6 20.3 %collective-permute-start.35 = (bf16[3,4,2,48,384]{4,3,2,1,0:T(8,128)(2,1)}, bf16[3,4,2,48,384]{4,3,2,1,0:T(8,128)(2,1)}, u32[]{:S(2)}, u32[]{:S(2)}) collective-permute-start(bf16[3,4,2,48,384]{4,3,2,1,0:T(8,128)(2,1)} %get-tuple-element.287), channel_id=1, source_target_pairs={{0,1},{1,0},{2,3},{3,2},{4,5},{5,4},{6,7},{7,6},{8,9},{9,8},{10,11... | collective-permute-start | bytes 2654216 | tf_op jit(solution)/shard_map/ppermute | solution.py:551
  279.6 20.3 %collective-permute-start.36 = (bf16[4,128,768]{2,1,0:T(8,128)(2,1)}, bf16[4,128,768]{2,1,0:T(8,128)(2,1)}, u32[]{:S(2)}, u32[]{:S(2)}) collective-permute-start(bf16[4,128,768]{2,1,0:T(8,128)(2,1)} %fusion.19), channel_id=1, source_target_pairs={{0,2},{1,3},{2,0},{3,1},{4,6},{5,7},{6,4},{7,5},{8,10},{9,11},{10,... | collective-permute-start | bytes 2359304 | tf_op jit(solution)/shard_map/ppermute | solution.py:547
  296.4 19.8 %collective-permute-start.42 = (bf16[256,768]{1,0:T(8,128)(2,1)}, bf16[256,768]{1,0:T(8,128)(2,1)}, u32[]{:S(2)}, u32[]{:S(2)}) collective-permute-start(bf16[256,768]{1,0:T(8,128)(2,1)} %get-tuple-element.300), channel_id=1, source_target_pairs={{0,16},{16,0},{1,17},{17,1},{2,18},{18,2},{3,19},{19,3},{4,20},{20... | collective-permute-start | bytes 1179656 | tf_op jit(solution)/shard_map/ppermute | solution.py:555
  308.5 44.9 %collective-permute-start.48 = (bf16[2,4,48,512]{3,2,1,0:T(8,128)(2,1)S(1)}, bf16[2,4,48,512]{3,2,1,0:T(8,128)(2,1)S(1)}, u32[]{:S(2)}, u32[]{:S(2)}) collective-permute-start(bf16[2,4,48,512]{3,2,1,0:T(8,128)(2,1)S(1)} %get-tuple-element.430), channel_id=1, source_target_pairs={{0,8},{1,9},{2,10},{3,11},{4,12},{5,13},{6,14},{7,15},{8,0},{9,1},... | collective-permute-start | bytes 1179656 | tf_op jit(solution)/shard_map/ppermute | solution.py:543
  313.4 40.1 %collective-permute-start.49 = (bf16[2,4,48,512]{3,2,1,0:T(8,128)(2,1)S(1)}, bf16[2,4,48,512]{3,2,1,0:T(8,128)(2,1)S(1)}, u32[]{:S(2)}, u32[]{:S(2)}) collective-permute-start(bf16[2,4,48,512]{3,2,1,0:T(8,128)(2,1)S(1)} %get-tuple-element.429), channel_id=1, source_target_pairs={{0,4},{1,5},{2,6},{3,7},{4,8},{5,9},{6,10},{7,11},{8,12},{9,13},{1... | collective-permute-start | bytes 1179656 | tf_op jit(solution)/shard_map/ppermute | solution.py:543
  332.2 21.2 %collective-permute-start.47 = (bf16[256,768]{1,0:T(8,128)(2,1)S(1)}, bf16[256,768]{1,0:T(8,128)(2,1)S(1)}, u32[]{:S(2)}, u32[]{:S(2)}) collective-permute-start(bf16[256,768]{1,0:T(8,128)(2,1)S(1)} %copy-done.29), channel_id=1, source_target_pairs={{16,0},{17,1},{18,2},{19,3},{20,4},{21,5},{22,6},{23,7},{24,8},{25... | collective-permute-start | bytes 1179656 | tf_op jit(solution)/shard_map/ppermute | solution.py:627
  (93 other events, 1106.0 us)
Sparse Core Ops, SparseCore 0:
  12.6 76.8 all-gather.5
  91.1 17.9 all-gather.7
  113.9 43.0 all-gather.9
  215.9 58.1 reduce-scatter.1

commit v2 on v1

--- a/solution.py
+++ b/solution.py
@@ -629,11 +629,10 @@
             passed, other = together(along_z(total, -1), other)
             if step == 1:
                 passed, shared, late = together(passed, shared, late)
-            if step == 0:
-                passed, late = together(passed, finish(late))
             here = add_all(mine, passed, other)
         total = here.astype(jnp.bfloat16)
-    return add_all(total, across_x(total)), shared, late
+    total, late = together(total, late)
+    return add_all(total, across_x(total)), shared, finish(late)
 
 
 def meta_rows(rows, width):

time: 384 us -> 381 us (level)
  no operation moved by 1% of the time
where the time goes in v2:
time: 381 us; the launch traced here: 380 us
  waiting for transfers between devices  128 us (34%)
  Pallas kernels  100 us (26%)
  starting transfers between devices  72.7 us (19%)
  other arithmetic  36.1 us (9%)
  local copies, waits for them, and re-layouts  24.5 us (6%)
  between operations  14.9 us (4%)
  matrix products  3.84 us (1%)
    ppermute x21, waiting for transfers between devices, along_z(): return lax.ppermute(values, 'shard', z_pairs(step))  87.9 us
    ppermute x21, starting transfers between devices, along_z(): return lax.ppermute(values, 'shard', z_pairs(step))  39 us
    pallas_call x1, Pallas kernels, run_experts(): pl.pallas_call(expert_kernel, name='run_experts', cost_estimate=busy(22),...  27.9 us
    pallas_call x2, Pallas kernels, attention_backward(): pl.pallas_call(attention_backward_kernel, name='attention_backward', cost...  24.8 us
    ppermute x18, starting transfers between devices, across_x(): return lax.ppermute(values, 'expert', [(0, 1), (1, 0)])  24.6 us
    ppermute x18, waiting for transfers between devices, across_x(): return lax.ppermute(values, 'expert', [(0, 1), (1, 0)])  16.6 us
    pallas_call x1, Pallas kernels, attention_forward(): pl.pallas_call(attention_forward_kernel, name='attention_forward', cost_e...  15.2 us
    pallas_call x1, Pallas kernels, weight_grads(): pl.pallas_call(weight_grad_kernel, name='weight_grads', cost_estimate=bus...  13.1 us
  transfers between devices with their start and end apart: 57, of which 21 were waited for; matrix products, arithmetic and copies ran while one was open for 14% of the time, Pallas kernels for 19%

profile of v2, /device:TPU:0, one launch (start us, length us, event | category | flops | bytes accessed | tf_op | source)
XLA Modules:
  0.0 379.8 jit_solution(7664271418340979567)
XLA Ops:
  14.4 3.1 collective-permute-start.1
  19.0 12.0 %collective-permute-done.1.refs_1_ = bf16[272,768]{1,0:T(8,128)(2,1)S(1)} collective-permute-done((bf16[272,768]{1,0:T(8,128)(2,1)S(1)}, bf16[272,768]{1,0:T(8,128)(2,1)S(1)}, u32[]{:S(2)}, u32[]{:S(2)}) %collective-permute-start.1) | collective-permute-done | bytes 417824 | tf_op jit(solution)/shard_map/ppermute | solution.py:543
  36.1 11.9 %collective-permute-done.3.refs_2_ = bf16[272,768]{1,0:T(8,128)(2,1)} collective-permute-done((bf16[272,768]{1,0:T(8,128)(2,1)S(1)}, bf16[272,768]{1,0:T(8,128)(2,1)}, u32[]{:S(2)}, u32[]{:S(2)}) %collective-permute-start.3) | collective-permute-done | bytes 417824 | tf_op jit(solution)/shard_map/ppermute | solution.py:543
  51.8 17.7 %collective-permute-done.5.refs_3_ = bf16[272,768]{1,0:T(8,128)(2,1)} collective-permute-done((bf16[272,768]{1,0:T(8,128)(2,1)}, bf16[272,768]{1,0:T(8,128)(2,1)}, u32[]{:S(2)}, u32[]{:S(2)}) %collective-permute-start.5) | collective-permute-done | bytes 417824 | tf_op jit(solution)/shard_map/ppermute | solution.py:543
  74.3 4.3 %collective-permute-done.7.refs_7_ = bf16[272,768]{1,0:T(8,128)(2,1)} collective-permute-done((bf16[272,768]{1,0:T(8,128)(2,1)}, bf16[272,768]{1,0:T(8,128)(2,1)}, u32[]{:S(2)}, u32[]{:S(2)}) %collective-permute-start.7) | collective-permute-done | bytes 417824 | tf_op jit(solution)/shard_map/ppermute | solution.py:555
  78.6 10.9 %all-gather.6.cloned.1.call-done.query_weight.key_weight.value_weight.output_weight = bf16[768,3200]{1,0:T(8,128)(2,1)} async-done(((bf16[48,3200]{1,0:T(8,128)(2,1)}), bf16[768,3200]{1,0:T(8,128)(2,1)}) %all-gather.6.cloned.1.call-update) | async-done | bytes 4915216 | tf_op jit(solution)/shard_map/all_gather | solution.py:1307
  97.4 15.2 %attention_forward.1 = (bf16[256,768]{1,0:T(8,128)(2,1)}, bf16[512,768]{1,0:T(8,128)(2,1)}, bf16[512,768]{1,0:T(8,128)(2,1)}, f32[256,768]{1,0:T(8,128)}, f32[6,256,128]{2,1,0:T(8,128)}, /*index=5*/f32[256,768]{1,0:T(8,128)}) custom-call(s32[4]{0:T(128)} %compare_select_fusion.4.place, bf16[512,768]{1,0:T(8,128)(2,1)} %fusion.2.normed_ref, ...), custom_call_target="tpu_custom_call" | custom-call | flops 6000000000 | bytes 45000000 | tf_op jit(solution)/shard_map/attention_forward/pallas_call | solution.py:1159
  117.0 8.0 %collective-permute-start.12 = (bf16[272,768]{1,0:T(8,128)(2,1)S(1)}, bf16[272,768]{1,0:T(8,128)(2,1)S(1)}, u32[]{:S(2)}, u32[]{:S(2)}) collective-permute-start(bf16[272,768]{1,0:T(8,128)(2,1)S(1)} %fusion.33.refs_0_), channel_id=1, source_target_pairs={{0,4},{1,5},{2,6},{3,7},{4,8},{5,9},{6,10},{7,11},{8,12},{9,13},{1... | collective-permute-start | bytes 1253384 | tf_op jit(solution)/shard_map/ppermute | solution.py:543
  126.5 7.7 %collective-permute-done.12.refs_1_ = bf16[272,768]{1,0:T(8,128)(2,1)S(1)} collective-permute-done((bf16[272,768]{1,0:T(8,128)(2,1)S(1)}, bf16[272,768]{1,0:T(8,128)(2,1)S(1)}, u32[]{:S(2)}, u32[]{:S(2)}) %collective-permute-start.12) | collective-permute-done | bytes 417824 | tf_op jit(solution)/shard_map/ppermute | solution.py:543
  138.7 7.9 %pick_slots.1 = (bf16[8,256,256]{2,1,0:T(8,128)(2,1)}, bf16[8,256,768]{2,1,0:T(8,128)(2,1)}) custom-call(s32[4]{0:T(128)} %compare_select_fusion.4.place, bf16[272,768]{1,0:T(8,128)(2,1)} %copy-done.26, bf16[272,768]{1,0:T(8,128)(2,1)} %copy-done.50, bf16[272,768]{1,0:T(8,128)(2,1)} %collective-permute-done.3.refs_2_, ...), custom_call_target="tpu_custom_call" | custom-call | flops 1600000000 | bytes 12000000 | tf_op jit(solution)/shard_map/pick_slots/pallas_call | solution.py:844
  150.3 10.2 %collective-permute-done.16.refs_3_ = bf16[272,768]{1,0:T(8,128)(2,1)S(1)} collective-permute-done((bf16[272,768]{1,0:T(8,128)(2,1)}, bf16[272,768]{1,0:T(8,128)(2,1)S(1)}, u32[]{:S(2)}, u32[]{:S(2)}) %collective-permute-start.16) | collective-permute-done | bytes 417824 | tf_op jit(solution)/shard_map/ppermute | solution.py:543
  162.1 11.3 %prepare_experts.1 = (f32[4,512,512]{2,1,0:T(8,128)}, bf16[4,768,1024]{2,1,0:T(8,128)(2,1)}, bf16[4,512,768]{2,1,0:T(8,128)(2,1)}) custom-call(s32[4]{0:T(128)} %compare_select_fusion.4.place, bf16[8,256,768]{2,1,0:T(8,128)(2,1)} %get-tuple-element.224.slot_ref.refs_1_, bf16[4,2,4,48,512]{4,3,2,1,0:T(8,128)(2,1)} %bitcast.247, ...), custom_call_target="tpu_custom_call" | custom-call | flops 4000000000 | bytes 30000000 | tf_op jit(solution)/shard_map/prepare_experts/pallas_call | solution.py:870
  173.5 27.9 %run_experts.1 = (bf16[8,256,768]{2,1,0:T(8,128)(2,1)}, bf16[4,512,512]{2,1,0:T(8,128)(2,1)}, bf16[4,512,1024]{2,1,0:T(8,128)(2,1)}, bf16[272,768]{1,0:T(8,128)(...) custom-call(s32[4]{0:T(128)} %compare_select_fusion.4.place, ...), custom_call_target="tpu_custom_call" | custom-call | flops 8800000000 | bytes 66000000 | tf_op jit(solution)/shard_map/run_experts/pallas_call | solution.py:907
  202.0 13.1 %weight_grads.1 = (bf16[4,4,2,4,48,512]{5,4,3,2,1,0:T(8,128)(2,1)}, bf16[2,4,128,768]{3,2,1,0:T(8,128)(2,1)}, bf16[2,4,128,768]{3,2,1,0:T(8,128)(2,1)}) custom-call(s32[4]{0:T(128)} %compare_select_fusion.4.place, bf16[8,256,768]{2,1,0:T(8,128)(2,1)} %get-tuple-element.236.refs_0_, bf16[8,256,768]{2,1,0:T(8,128)(2,1)} %get-tuple-element.224.slot_ref.refs_1_, ...), custom_call_target="tpu_custom_call" | custom-call | flops 4800000000 | bytes 36000000 | tf_op jit(solution)/shard_map/weight_grads/pallas_call | solution.py:947
  221.6 6.4 %collective-permute-done.23 = bf16[272,768]{1,0:T(8,128)(2,1)S(1)} collective-permute-done((bf16[272,768]{1,0:T(8,128)(2,1)}, bf16[272,768]{1,0:T(8,128)(2,1)S(1)}, u32[]{:S(2)}, u32[]{:S(2)}) %collective-permute-start.23) | collective-permute-done | bytes 417824 | tf_op jit(solution)/shard_map/ppermute | solution.py:555
  228.2 3.8 collective-permute-start.24
  237.9 4.3 %collective-permute-start.26 = (bf16[272,768]{1,0:T(8,128)(2,1)S(1)}, bf16[272,768]{1,0:T(8,128)(2,1)S(1)}, u32[]{:S(2)}, u32[]{:S(2)}) collective-permute-start(bf16[272,768]{1,0:T(8,128)(2,1)S(1)} %add_convert_fusion.4), channel_id=1, source_target_pairs={{0,12},{1,13},{2,14},{3,15},{4,0},{5,1},{6,2},{7,3},{8,4},{9,5},{1... | collective-permute-start | bytes 1253384 | tf_op jit(solution)/shard_map/ppermute | solution.py:543
  259.6 12.4 %attention_backward.2 = (bf16[3,4,2,48,384]{4,3,2,1,0:T(8,128)(2,1)}, bf16[3,4,2,48,384]{4,3,2,1,0:T(8,128)(2,1)}, f32[512,768]{1,0:T(8,128)}) custom-call(s32[4]{0:T(128)} %compare_select_fusion.4.place, bf16[512,768]{1,0:T(8,128)(2,1)} %fusion.2.normed_ref, ...), custom_call_target="tpu_custom_call" | custom-call | flops 5600000000 | bytes 42000000 | tf_op jit(solution)/shard_map/attention_backward/pallas_call | solution.py:1196
  282.5 12.3 %attention_backward.3 = (bf16[3,4,2,48,384]{4,3,2,1,0:T(8,128)(2,1)}, bf16[3,4,2,48,384]{4,3,2,1,0:T(8,128)(2,1)}, f32[512,768]{1,0:T(8,128)}) custom-call(s32[4]{0:T(128)} %compare_select_fusion.4.place, bf16[512,768]{1,0:T(8,128)(2,1)} %fusion.2.normed_ref, ...), custom_call_target="tpu_custom_call" | custom-call | flops 5600000000 | bytes 42000000 | tf_op jit(solution)/shard_map/attention_backward/pallas_call | solution.py:1196
  310.5 2.8 bitcast_add_fusion
  317.7 8.0 %collective-permute-done.40 = bf16[48,3200]{1,0:T(8,128)(2,1)S(1)} collective-permute-done((bf16[48,3200]{1,0:T(8,128)(2,1)S(1)}, bf16[48,3200]{1,0:T(8,128)(2,1)S(1)}, u32[]{:S(2)}, u32[]{:S(2)}) %collective-permute-start.40) | collective-permute-done | bytes 307232 | tf_op jit(solution)/shard_map/ppermute | solution.py:547
  333.5 10.5 %collective-permute-done.43 = bf16[48,3200]{1,0:T(8,128)(2,1)S(1)} collective-permute-done((bf16[48,3200]{1,0:T(8,128)(2,1)S(1)}, bf16[48,3200]{1,0:T(8,128)(2,1)S(1)}, u32[]{:S(2)}, u32[]{:S(2)}) %collective-permute-start.43) | collective-permute-done | bytes 307232 | tf_op jit(solution)/shard_map/ppermute | solution.py:543
  345.3 8.2 %collective-permute-done.45 = bf16[48,3200]{1,0:T(8,128)(2,1)S(1)} collective-permute-done((bf16[48,3200]{1,0:T(8,128)(2,1)S(1)}, bf16[48,3200]{1,0:T(8,128)(2,1)S(1)}, u32[]{:S(2)}, u32[]{:S(2)}) %collective-permute-start.45) | collective-permute-done | bytes 307232 | tf_op jit(solution)/shard_map/ppermute | solution.py:543
  357.9 4.4 %collective-permute-done.50 = bf16[48,3200]{1,0:T(8,128)(2,1)S(1)} collective-permute-done((bf16[48,3200]{1,0:T(8,128)(2,1)S(1)}, bf16[48,3200]{1,0:T(8,128)(2,1)S(1)}, u32[]{:S(2)}, u32[]{:S(2)}) %collective-permute-start.50) | collective-permute-done | bytes 307232 | tf_op jit(solution)/shard_map/ppermute | solution.py:543
  (341 shorter events, 130.4 us)
Async XLA Ops:
  7.2 82.3 %all-gather.6.cloned.1.call-start = ((), (), s32[]{:S(2)}) async-start(), calls=%async_computation.1 | async-start | bytes 5222400 | tf_op jit(solution)/shard_map/all_gather | solution.py:1307
  12.5 149.6 %all-gather.8.cloned.1.call-start = ((), (), s32[]{:S(2)}) async-start(), calls=%async_computation.3 | async-start | bytes 1966080 | tf_op jit(solution)/shard_map/all_gather | solution.py:604
  34.6 54.9 %collective-permute-start.8 = (bf16[4,128,768]{2,1,0:T(8,128)(2,1)}, bf16[4,128,768]{2,1,0:T(8,128)(2,1)}, u32[]{:S(2)}, u32[]{:S(2)}) collective-permute-start(bf16[4,128,768]{2,1,0:T(8,128)(2,1)} %refs_0_.1), channel_id=1, source_target_pairs={{0,2},{1,3},{2,0},{3,1},{4,6},{5,7},{6,4},{7,5},{8,10},{9,11},{10,... | collective-permute-start | bytes 2359304 | tf_op jit(solution)/shard_map/ppermute | solution.py:547
  48.1 21.4 %collective-permute-start.5 = (bf16[272,768]{1,0:T(8,128)(2,1)}, bf16[272,768]{1,0:T(8,128)(2,1)}, u32[]{:S(2)}, u32[]{:S(2)}) collective-permute-start(bf16[272,768]{1,0:T(8,128)(2,1)} %collective-permute-done.3.refs_2_), channel_id=1, source_target_pairs={{0,4},{1,5},{2,6},{3,7},{4,8},{5,9},{6,10},{7,11},{8,12},{9,13},{1... | collective-permute-start | bytes 1253384 | tf_op jit(solution)/shard_map/ppermute | solution.py:543
  48.1 21.4 %collective-permute-start.6 = (bf16[272,768]{1,0:T(8,128)(2,1)}, bf16[272,768]{1,0:T(8,128)(2,1)S(1)}, u32[]{:S(2)}, u32[]{:S(2)}) collective-permute-start(bf16[272,768]{1,0:T(8,128)(2,1)} %collective-permute-done.3.refs_2_), channel_id=1, source_target_pairs={{0,16},{16,0},{1,17},{17,1},{2,18},{18,2},{3,19},{19,3},{4,20},{20... | collective-permute-start | bytes 1253384 | tf_op jit(solution)/shard_map/ppermute | solution.py:555
  49.9 39.6 %collective-permute-start.9 = (bf16[2,4,48,512]{3,2,1,0:T(8,128)(2,1)S(1)}, bf16[2,4,48,512]{3,2,1,0:T(8,128)(2,1)S(1)}, u32[]{:S(2)}, u32[]{:S(2)}) collective-permute-start(bf16[2,4,48,512]{3,2,1,0:T(8,128)(2,1)S(1)} %pad_maximum_fusion.3), channel_id=1, source_target_pairs={{0,4},{1,5},{2,6},{3,7},{4,8},{5,9},{6,10},{7,11},{8,12},{9,13},{1... | collective-permute-start | bytes 1179656 | tf_op jit(solution)/shard_map/ppermute | solution.py:543
  51.2 23.1 %collective-permute-start = (bf16[256,768]{1,0:T(8,128)(2,1)S(1)}, bf16[256,768]{1,0:T(8,128)(2,1)S(1)}, u32[]{:S(2)}, u32[]{:S(2)}) collective-permute-start(bf16[256,768]{1,0:T(8,128)(2,1)S(1)} %bitcast.229), channel_id=1, source_target_pairs={{0,16},{16,0},{1,17},{17,1},{2,18},{18,2},{3,19},{19,3},{4,20},{20... | collective-permute-start | bytes 1179656 | tf_op jit(solution)/shard_map/ppermute | solution.py:555
  89.5 72.6 %all-gather.10.cloned.1.call-start = ((), (), s32[]{:S(2)}) async-start(), calls=%async_computation.4 | async-start | bytes 5898240 | tf_op jit(solution)/shard_map/all_gather | solution.py:604
  91.6 21.0 %collective-permute-start.10 = (bf16[2,4,48,512]{3,2,1,0:T(8,128)(2,1)S(1)}, bf16[2,4,48,512]{3,2,1,0:T(8,128)(2,1)S(1)}, u32[]{:S(2)}, u32[]{:S(2)}) collective-permute-start(bf16[2,4,48,512]{3,2,1,0:T(8,128)(2,1)S(1)} %pad_maximum_fusion.4), channel_id=1, source_target_pairs={{0,8},{1,9},{2,10},{3,11},{4,12},{5,13},{6,14},{7,15},{8,0},{9,1},... | collective-permute-start | bytes 1179656 | tf_op jit(solution)/shard_map/ppermute | solution.py:543
  92.2 20.4 %collective-permute-start.11 = (bf16[2,4,48,512]{3,2,1,0:T(8,128)(2,1)S(1)}, bf16[2,4,48,512]{3,2,1,0:T(8,128)(2,1)S(1)}, u32[]{:S(2)}, u32[]{:S(2)}) collective-permute-start(bf16[2,4,48,512]{3,2,1,0:T(8,128)(2,1)S(1)} %pad_maximum_fusion.5), channel_id=1, source_target_pairs={{0,12},{1,13},{2,14},{3,15},{4,0},{5,1},{6,2},{7,3},{8,4},{9,5},{1... | collective-permute-start | bytes 1179656 | tf_op jit(solution)/shard_map/ppermute | solution.py:543
  113.8 161.2 %reduce-scatter.2.cloned.1.call-start = ((), (), s32[]{:S(2)}) async-start(), calls=%async_computation.2 | async-start | bytes 7864320 | tf_op jit(solution)/shard_map/reduce_scatter | solution.py:598
  138.2 23.9 %collective-permute-start.19 = (bf16[4,128,768]{2,1,0:T(8,128)(2,1)S(1)}, bf16[4,128,768]{2,1,0:T(8,128)(2,1)}, u32[]{:S(2)}, u32[]{:S(2)}) collective-permute-start(bf16[4,128,768]{2,1,0:T(8,128)(2,1)S(1)} %copy-done.49), channel_id=1, source_target_pairs={{0,1},{1,0},{2,3},{3,2},{4,5},{5,4},{6,7},{7,6},{8,9},{9,8},{10,11... | collective-permute-start | bytes 2359304 | tf_op jit(solution)/shard_map/ppermute | solution.py:551
  138.2 23.9 %collective-permute-start.20 = (bf16[4,128,768]{2,1,0:T(8,128)(2,1)}, bf16[4,128,768]{2,1,0:T(8,128)(2,1)}, u32[]{:S(2)}, u32[]{:S(2)}) collective-permute-start(bf16[4,128,768]{2,1,0:T(8,128)(2,1)} %collective-permute-done.8.refs_1_), channel_id=1, source_target_pairs={{0,1},{1,0},{2,3},{3,2},{4,5},{5,4},{6,7},{7,6},{8,9},{9,8},{10,11... | collective-permute-start | bytes 2359304 | tf_op jit(solution)/shard_map/ppermute | solution.py:551
  242.9 29.8 %collective-permute-start.32 = (bf16[2,4,128,768]{3,2,1,0:T(8,128)(2,1)}, bf16[2,4,128,768]{3,2,1,0:T(8,128)(2,1)}, u32[]{:S(2)}, u32[]{:S(2)}) collective-permute-start(bf16[2,4,128,768]{3,2,1,0:T(8,128)(2,1)} %get-tuple-element.279), channel_id=1, source_target_pairs={{0,1},{1,0},{2,3},{3,2},{4,5},{5,4},{6,7},{7,6},{8,9},{9,8},{10,11... | collective-permute-start | bytes 4718600 | tf_op jit(solution)/shard_map/ppermute | solution.py:551
  245.1 29.8 %collective-permute-start.30 = (bf16[256,768]{1,0:T(8,128)(2,1)}, bf16[256,768]{1,0:T(8,128)(2,1)}, u32[]{:S(2)}, u32[]{:S(2)}) collective-permute-start(bf16[256,768]{1,0:T(8,128)(2,1)} %get-tuple-element.275), channel_id=1, source_target_pairs={{0,16},{16,0},{1,17},{17,1},{2,18},{18,2},{3,19},{19,3},{4,20},{20... | collective-permute-start | bytes 1179656 | tf_op jit(solution)/shard_map/ppermute | solution.py:555
  245.2 51.2 %collective-permute-start.34 = (bf16[256,768]{1,0:T(8,128)(2,1)}, bf16[256,768]{1,0:T(8,128)(2,1)}, u32[]{:S(2)}, u32[]{:S(2)}) collective-permute-start(bf16[256,768]{1,0:T(8,128)(2,1)} %get-tuple-element.289), channel_id=1, source_target_pairs={{0,16},{16,0},{1,17},{17,1},{2,18},{18,2},{3,19},{19,3},{4,20},{20... | collective-permute-start | bytes 1179656 | tf_op jit(solution)/shard_map/ppermute | solution.py:555
  256.0 19.0 %collective-permute-start.29 = (bf16[256,768]{1,0:T(8,128)(2,1)}, bf16[256,768]{1,0:T(8,128)(2,1)}, u32[]{:S(2)}, u32[]{:S(2)}) collective-permute-start(bf16[256,768]{1,0:T(8,128)(2,1)} %add_convert_fusion.10), channel_id=1, source_target_pairs={{0,12},{1,13},{2,14},{3,15},{4,0},{5,1},{6,2},{7,3},{8,4},{9,5},{1... | collective-permute-start | bytes 1179656 | tf_op jit(solution)/shard_map/ppermute | solution.py:543
  277.3 20.6 %collective-permute-start.33 = (bf16[256,768]{1,0:T(8,128)(2,1)}, bf16[256,768]{1,0:T(8,128)(2,1)}, u32[]{:S(2)}, u32[]{:S(2)}) collective-permute-start(bf16[256,768]{1,0:T(8,128)(2,1)} %add_convert_fusion.9), channel_id=1, source_target_pairs={{0,12},{1,13},{2,14},{3,15},{4,0},{5,1},{6,2},{7,3},{8,4},{9,5},{1... | collective-permute-start | bytes 1179656 | tf_op jit(solution)/shard_map/ppermute | solution.py:543
  279.6 20.3 %collective-permute-start.35 = (bf16[3,4,2,48,384]{4,3,2,1,0:T(8,128)(2,1)}, bf16[3,4,2,48,384]{4,3,2,1,0:T(8,128)(2,1)}, u32[]{:S(2)}, u32[]{:S(2)}) collective-permute-start(bf16[3,4,2,48,384]{4,3,2,1,0:T(8,128)(2,1)} %get-tuple-element.290), channel_id=1, source_target_pairs={{0,1},{1,0},{2,3},{3,2},{4,5},{5,4},{6,7},{7,6},{8,9},{9,8},{10,11... | collective-permute-start | bytes 2654216 | tf_op jit(solution)/shard_map/ppermute | solution.py:551
  279.6 20.3 %collective-permute-start.36 = (bf16[4,128,768]{2,1,0:T(8,128)(2,1)}, bf16[4,128,768]{2,1,0:T(8,128)(2,1)}, u32[]{:S(2)}, u32[]{:S(2)}) collective-permute-start(bf16[4,128,768]{2,1,0:T(8,128)(2,1)} %fusion.19), channel_id=1, source_target_pairs={{0,2},{1,3},{2,0},{3,1},{4,6},{5,7},{6,4},{7,5},{8,10},{9,11},{10,... | collective-permute-start | bytes 2359304 | tf_op jit(solution)/shard_map/ppermute | solution.py:547
  296.4 19.8 %collective-permute-start.42 = (bf16[256,768]{1,0:T(8,128)(2,1)}, bf16[256,768]{1,0:T(8,128)(2,1)}, u32[]{:S(2)}, u32[]{:S(2)}) collective-permute-start(bf16[256,768]{1,0:T(8,128)(2,1)} %get-tuple-element.303), channel_id=1, source_target_pairs={{0,16},{16,0},{1,17},{17,1},{2,18},{18,2},{3,19},{19,3},{4,20},{20... | collective-permute-start | bytes 1179656 | tf_op jit(solution)/shard_map/ppermute | solution.py:555
  308.6 44.9 %collective-permute-start.48 = (bf16[2,4,48,512]{3,2,1,0:T(8,128)(2,1)S(1)}, bf16[2,4,48,512]{3,2,1,0:T(8,128)(2,1)S(1)}, u32[]{:S(2)}, u32[]{:S(2)}) collective-permute-start(bf16[2,4,48,512]{3,2,1,0:T(8,128)(2,1)S(1)} %get-tuple-element.434), channel_id=1, source_target_pairs={{0,8},{1,9},{2,10},{3,11},{4,12},{5,13},{6,14},{7,15},{8,0},{9,1},... | collective-permute-start | bytes 1179656 | tf_op jit(solution)/shard_map/ppermute | solution.py:543
  313.4 40.1 %collective-permute-start.49 = (bf16[2,4,48,512]{3,2,1,0:T(8,128)(2,1)S(1)}, bf16[2,4,48,512]{3,2,1,0:T(8,128)(2,1)S(1)}, u32[]{:S(2)}, u32[]{:S(2)}) collective-permute-start(bf16[2,4,48,512]{3,2,1,0:T(8,128)(2,1)S(1)} %get-tuple-element.433), channel_id=1, source_target_pairs={{0,4},{1,5},{2,6},{3,7},{4,8},{5,9},{6,10},{7,11},{8,12},{9,13},{1... | collective-permute-start | bytes 1179656 | tf_op jit(solution)/shard_map/ppermute | solution.py:543
  332.2 21.3 %collective-permute-start.47 = (bf16[256,768]{1,0:T(8,128)(2,1)S(1)}, bf16[256,768]{1,0:T(8,128)(2,1)S(1)}, u32[]{:S(2)}, u32[]{:S(2)}) collective-permute-start(bf16[256,768]{1,0:T(8,128)(2,1)S(1)} %copy-done.30), channel_id=1, source_target_pairs={{16,0},{17,1},{18,2},{19,3},{20,4},{21,5},{22,6},{23,7},{24,8},{25... | collective-permute-start | bytes 1179656 | tf_op jit(solution)/shard_map/ppermute | solution.py:627
  (93 other events, 1092.1 us)
Sparse Core Ops, SparseCore 0:
  12.6 76.8 all-gather.5
  91.1 17.9 all-gather.7
  113.9 43.0 all-gather.9
  215.9 58.1 reduce-scatter.1
